TPU v7x, 32 devices: a whole 2x2x4 slice. The times are simulated.
32 devices in a mesh: ctx: 8 (over z, y), ch: 4 (over x, core).
Axes of the slice: x: 2, y: 2, z: 4, core: 2. Of those that a mesh axis runs over, the one named last changes fastest.
Arguments:
- query_short: bfloat16 [2048, 8192], P('ctx', 'ch'), may hold values from -6 to 6
- key_short: bfloat16 [2048, 8192], P('ctx', 'ch'), may hold values from -6 to 6
- value_short: bfloat16 [2048, 8192], P('ctx', 'ch'), may hold values from -6 to 6
- grad_short: bfloat16 [2048, 8192], P('ctx', 'ch'), may hold values from -10 to 10
- query_medium: bfloat16 [2048, 8192], P('ctx', 'ch'), may hold values from -6 to 6
- key_medium: bfloat16 [2048, 8192], P('ctx', 'ch'), may hold values from -6 to 6
- value_medium: bfloat16 [2048, 8192], P('ctx', 'ch'), may hold values from -6 to 6
- grad_medium: bfloat16 [2048, 8192], P('ctx', 'ch'), may hold values from -10 to 10
- query_long: bfloat16 [2048, 8192], P('ctx', 'ch'), may hold values from -6 to 6
- key_long: bfloat16 [2048, 8192], P('ctx', 'ch'), may hold values from -8 to 8
- value_long: bfloat16 [2048, 8192], P('ctx', 'ch'), may hold values from -8 to 8
- grad_long: bfloat16 [2048, 8192], P('ctx', 'ch'), may hold values from -10 to 10
- taps_short: float32 [7, 8192], P(None, 'ch'), may hold values from -2 to 2
- taps_medium: float32 [128, 8192], P(None, 'ch'), may hold values from -0.5 to 0.5
- residues: float32 [16, 8192], P(None, 'ch'), may hold values from -1.5 to 1.5
- decay_rates: float32 [16, 8192], P(None, 'ch'), may hold values from 2.4414063e-05 to 0.07
Outputs:
- query_grad_short: bfloat16 [2048, 8192], P('ctx', 'ch')
- key_grad_short: bfloat16 [2048, 8192], P('ctx', 'ch')
- value_grad_short: bfloat16 [2048, 8192], P('ctx', 'ch')
- query_grad_medium: bfloat16 [2048, 8192], P('ctx', 'ch')
- key_grad_medium: bfloat16 [2048, 8192], P('ctx', 'ch')
- value_grad_medium: bfloat16 [2048, 8192], P('ctx', 'ch')
- query_grad_long: bfloat16 [2048, 8192], P('ctx', 'ch')
- key_grad_long: bfloat16 [2048, 8192], P('ctx', 'ch')
- value_grad_long: bfloat16 [2048, 8192], P('ctx', 'ch')
- taps_short_grad: float32 [7, 8192], P(None, 'ch')
- taps_medium_grad: float32 [128, 8192], P(None, 'ch')
- residue_grad: float32 [16, 8192], P(None, 'ch')
All inputs are finite; a program needn't handle non-finite values.
Results may differ from a plain program's by a relative error of at most 0.008.
Values may be sent and summed in bfloat16 or wider, within the bound.
A program may use at most 128 MiB of HBM per device.

v0:
```python
import jax
import jax.numpy as jnp
from jax import lax
from jax.sharding import PartitionSpec as P


def from_behind(value, axis, steps):
    count = lax.axis_size(axis)
    first, last = (max(0, -steps), min(count, count - steps))
    return lax.ppermute(value, axis, [(source, source + steps) for source in range(first, last)])


def depthwise(signal, kernel):
    result = lax.conv_general_dilated(
        signal[None],
        kernel[:, None, :],
        (1,),
        "VALID",
        dimension_numbers=("NWC", "WIO", "NWC"),
        feature_group_count=signal.shape[1],
        precision=lax.Precision.HIGHEST,
    )
    return result[0]


def elementwise(first, second):
    return (first.astype(jnp.float32) * second.astype(jnp.float32)).astype(jnp.bfloat16)


def explicit_filter(product, before, signal, after, taps):
    padded = jnp.concatenate([before, product], 0).astype(jnp.float32)
    forward = depthwise(padded, taps[::-1])
    trailing = jnp.concatenate([signal, after], 0).astype(jnp.float32)
    backward = depthwise(trailing, taps)
    tap_sums = depthwise(padded, signal.astype(jnp.float32))[::-1]
    return (forward, backward, tap_sums)


def operator_grads(keys, values, grad, forward, backward):
    query_grad = (grad.astype(jnp.float32) * forward).astype(jnp.bfloat16)
    key_grad = (backward * values.astype(jnp.float32)).astype(jnp.bfloat16)
    value_grad = (backward * keys.astype(jnp.float32)).astype(jnp.bfloat16)
    return (query_grad, key_grad, value_grad)


def long_local(product_f, signal_f, weights, amplitudes, decay_rates):
    length = product_f.shape[0]
    rows = lax.broadcasted_iota(jnp.int32, (length, length), 0)
    columns = lax.broadcasted_iota(jnp.int32, (length, length), 1)
    lower = (rows >= columns).astype(jnp.float32)
    upper = (rows <= columns).astype(jnp.float32)
    places = jnp.arange(length, dtype=jnp.float32)[:, None]

    def one_mode(totals, inputs):
        rate, weight, amplitude = inputs
        grow = jnp.exp(rate[None, :] * places)
        shrink = jnp.exp(-rate[None, :] * places)
        state = shrink * jnp.dot(lower, grow * product_f, precision=lax.Precision.HIGHEST)
        reverse = grow * jnp.dot(upper, shrink * signal_f, precision=lax.Precision.HIGHEST)
        totals = (totals[0] + weight[None, :] * state, totals[1] + weight[None, :] * reverse)
        return (totals, (state[length - 1], reverse[0], amplitude * jnp.sum(signal_f * state, 0)))

    zeros = jnp.zeros(product_f.shape, jnp.float32)
    totals, outputs = lax.scan(one_mode, (zeros, zeros), (decay_rates, weights, amplitudes))
    return (totals[0], totals[1], outputs[0], outputs[1], outputs[2])


def long_carry(
    forward, backward, residue_part, signal_f, carry_in, carry_out, weights, amplitudes, decay_rates
):
    length = forward.shape[0]
    places = jnp.arange(length, dtype=jnp.float32)[:, None]

    def one_mode(totals, inputs):
        rate, weight, amplitude, entering, leaving = inputs
        fade_in = jnp.exp(-rate[None, :] * (places + 1.0))
        fade_back = jnp.exp(-rate[None, :] * (length - places))
        totals = (
            totals[0] + weight[None, :] * fade_in * entering[None, :],
            totals[1] + weight[None, :] * fade_back * leaving[None, :],
        )
        return (totals, amplitude * entering * jnp.sum(signal_f * fade_in, 0))

    totals, extra = lax.scan(
        one_mode, (forward, backward), (decay_rates, weights, amplitudes, carry_in, carry_out)
    )
    return (totals[0], totals[1], residue_part + extra)


def body(
    query_short,
    key_short,
    value_short,
    grad_short,
    query_medium,
    key_medium,
    value_medium,
    grad_medium,
    query_long,
    key_long,
    value_long,
    grad_long,
    taps_short,
    taps_medium,
    residues,
    decay_rates,
):
    length = query_short.shape[0]
    short_len = taps_short.shape[0]
    medium_len = taps_medium.shape[0]
    product_short = elementwise(key_short, value_short)
    product_medium = elementwise(key_medium, value_medium)
    product_long = elementwise(key_long, value_long)
    signal_short = elementwise(grad_short, query_short)
    signal_medium = elementwise(grad_medium, query_medium)
    signal_long = elementwise(grad_long, query_long)
    tails = jnp.concatenate(
        [product_short[length - short_len + 1 :], product_medium[length - medium_len + 1 :]], 0
    )
    before = from_behind(tails, "ctx", 1)
    heads = jnp.concatenate([signal_short[: short_len - 1], signal_medium[: medium_len - 1]], 0)
    after = from_behind(heads, "ctx", -1)
    amplitudes = jnp.sqrt(-jnp.expm1(-2.0 * decay_rates))
    weights = amplitudes * residues
    product_f = product_long.astype(jnp.float32)
    signal_f = signal_long.astype(jnp.float32)
    forward_long, backward_long, ends, starts, residue_part = long_local(
        product_f, signal_f, weights, amplitudes, decay_rates
    )
    forward_short, backward_short, raw_short = explicit_filter(
        product_short, before[: short_len - 1], signal_short, after[: short_len - 1], taps_short
    )
    forward_medium, backward_medium, raw_medium = explicit_filter(
        product_medium, before[short_len - 1 :], signal_medium, after[short_len - 1 :], taps_medium
    )
    every_end, every_start = (
        lax.all_gather(ends[None], "ctx", axis=0, tiled=True),
        lax.all_gather(starts[None], "ctx", axis=0, tiled=True),
    )
    count = lax.axis_size("ctx")
    index = lax.axis_index("ctx")
    blocks = jnp.arange(count, dtype=jnp.int32)[:, None, None]
    earlier = blocks < index
    later = blocks > index
    gap_before = jnp.where(earlier, index - 1 - blocks, 0).astype(jnp.float32)
    gap_after = jnp.where(later, blocks - index - 1, 0).astype(jnp.float32)
    scaled = decay_rates[None] * length
    carry_in = jnp.sum(jnp.where(earlier, jnp.exp(-scaled * gap_before) * every_end, 0.0), 0)
    carry_out = jnp.sum(jnp.where(later, jnp.exp(-scaled * gap_after) * every_start, 0.0), 0)
    forward_long, backward_long, raw_residue = long_carry(
        forward_long,
        backward_long,
        residue_part,
        signal_f,
        carry_in,
        carry_out,
        weights,
        amplitudes,
        decay_rates,
    )
    grads_short = operator_grads(key_short, value_short, grad_short, forward_short, backward_short)
    grads_medium = operator_grads(
        key_medium, value_medium, grad_medium, forward_medium, backward_medium
    )
    grads_long = operator_grads(key_long, value_long, grad_long, forward_long, backward_long)
    summed_short, summed_medium, summed_residue = lax.psum(
        (raw_short, raw_medium, raw_residue), "ctx"
    )
    squares = (
        jnp.sum(summed_short * summed_short)
        + jnp.sum(summed_medium * summed_medium)
        + jnp.sum(summed_residue * summed_residue)
    )
    total = lax.psum(squares, "ch")
    entries = (short_len + medium_len + residues.shape[0]) * residues.shape[1] * lax.axis_size("ch")
    factor = 1.0 / jnp.sqrt(total / entries + 1e-06)
    return (
        grads_short[0],
        grads_short[1],
        grads_short[2],
        grads_medium[0],
        grads_medium[1],
        grads_medium[2],
        grads_long[0],
        grads_long[1],
        grads_long[2],
        factor * summed_short,
        factor * summed_medium,
        factor * summed_residue,
    )


def solution(mesh):
    in_specs = (
        P("ctx", "ch"),
        P("ctx", "ch"),
        P("ctx", "ch"),
        P("ctx", "ch"),
        P("ctx", "ch"),
        P("ctx", "ch"),
        P("ctx", "ch"),
        P("ctx", "ch"),
        P("ctx", "ch"),
        P("ctx", "ch"),
        P("ctx", "ch"),
        P("ctx", "ch"),
        P(None, "ch"),
        P(None, "ch"),
        P(None, "ch"),
        P(None, "ch"),
    )
    out_specs = (
        P("ctx", "ch"),
        P("ctx", "ch"),
        P("ctx", "ch"),
        P("ctx", "ch"),
        P("ctx", "ch"),
        P("ctx", "ch"),
        P("ctx", "ch"),
        P("ctx", "ch"),
        P("ctx", "ch"),
        P(None, "ch"),
        P(None, "ch"),
        P(None, "ch"),
    )
    return jax.shard_map(body, mesh=mesh, in_specs=in_specs, out_specs=out_specs, check_vma=False)
```

profile of v0, /device:TPU:0, one launch (start us, length us, event | category | flops | bytes accessed | tf_op | source)
XLA Modules:
  0.0 715.3 jit_solution(15044254287578084914)
XLA Ops:
  13.9 4.3 fusion.59
  18.9 277.9 %while.37 = (s32[]{:T(128)}, f32[256,2048]{1,0:T(8,128)}, f32[256,2048]{1,0:T(8,128)}, f32[16,2048]{1,0:T(8,128)S(1)}, f32[16,2048]{1,0:T(8,128)}, /*index=5*/f3...) while((s32[]{:T(128)}, f32[256,2048]{1,0:T(8,128)}, ...), condition=%wide.region_2.3_spmd.clone.clone, body=%wide.region_0.2_spmd.clone.clone.sunk | while | flops 3229878272 | bytes 21176496 | solution.py:64
  19.8 3.8 fusion.82
  23.7 7.8 %multiply_reduce_fusion.8 = (f32[2048]{0:T(1024)S(1)}, f32[256,2048]{1,0:T(8,128)}, f32[256,2048]{1,0:T(8,128)}, f32[256,2048]{1,0:T(8,128)}) fusion(f32[256,2048]{1,0:T(8,128)S(1)} %get-tuple-element.547, f32[2048]{0:T(1024)S(1)} %bitcast.100, f32[256,2048]{1,0:T(8,128)} %get-tuple-element.526, pred[]{:T(512)S(6)} %compare.26, ...), kind=kOutput, calls=%fused_computation.27.clone.1 | convolution fusion | flops 1617033216 | bytes 16809984 | tf_op jit(solution)/shard_map/while/body/eval_jaxpr/dot_general | solution.py:58
  36.0 3.8 fusion.82
  39.9 9.1 %multiply_reduce_fusion.8 = (f32[2048]{0:T(1024)S(1)}, f32[256,2048]{1,0:T(8,128)}, f32[256,2048]{1,0:T(8,128)}, f32[256,2048]{1,0:T(8,128)}) fusion(f32[256,2048]{1,0:T(8,128)S(1)} %get-tuple-element.547, f32[2048]{0:T(1024)S(1)} %bitcast.100, f32[256,2048]{1,0:T(8,128)} %get-tuple-element.526, pred[]{:T(512)S(6)} %compare.26, ...), kind=kOutput, calls=%fused_computation.27.clone.1 | convolution fusion | flops 1617033216 | bytes 16809984 | tf_op jit(solution)/shard_map/while/body/eval_jaxpr/dot_general | solution.py:58
  53.5 3.8 fusion.82
  57.3 9.1 %multiply_reduce_fusion.8 = (f32[2048]{0:T(1024)S(1)}, f32[256,2048]{1,0:T(8,128)}, f32[256,2048]{1,0:T(8,128)}, f32[256,2048]{1,0:T(8,128)}) fusion(f32[256,2048]{1,0:T(8,128)S(1)} %get-tuple-element.547, f32[2048]{0:T(1024)S(1)} %bitcast.100, f32[256,2048]{1,0:T(8,128)} %get-tuple-element.526, pred[]{:T(512)S(6)} %compare.26, ...), kind=kOutput, calls=%fused_computation.27.clone.1 | convolution fusion | flops 1617033216 | bytes 16809984 | tf_op jit(solution)/shard_map/while/body/eval_jaxpr/dot_general | solution.py:58
  70.9 3.8 fusion.82
  74.8 9.1 %multiply_reduce_fusion.8 = (f32[2048]{0:T(1024)S(1)}, f32[256,2048]{1,0:T(8,128)}, f32[256,2048]{1,0:T(8,128)}, f32[256,2048]{1,0:T(8,128)}) fusion(f32[256,2048]{1,0:T(8,128)S(1)} %get-tuple-element.547, f32[2048]{0:T(1024)S(1)} %bitcast.100, f32[256,2048]{1,0:T(8,128)} %get-tuple-element.526, pred[]{:T(512)S(6)} %compare.26, ...), kind=kOutput, calls=%fused_computation.27.clone.1 | convolution fusion | flops 1617033216 | bytes 16809984 | tf_op jit(solution)/shard_map/while/body/eval_jaxpr/dot_general | solution.py:58
  88.4 3.8 fusion.82
  92.2 9.1 %multiply_reduce_fusion.8 = (f32[2048]{0:T(1024)S(1)}, f32[256,2048]{1,0:T(8,128)}, f32[256,2048]{1,0:T(8,128)}, f32[256,2048]{1,0:T(8,128)}) fusion(f32[256,2048]{1,0:T(8,128)S(1)} %get-tuple-element.547, f32[2048]{0:T(1024)S(1)} %bitcast.100, f32[256,2048]{1,0:T(8,128)} %get-tuple-element.526, pred[]{:T(512)S(6)} %compare.26, ...), kind=kOutput, calls=%fused_computation.27.clone.1 | convolution fusion | flops 1617033216 | bytes 16809984 | tf_op jit(solution)/shard_map/while/body/eval_jaxpr/dot_general | solution.py:58
  105.8 3.8 fusion.82
  109.7 9.1 %multiply_reduce_fusion.8 = (f32[2048]{0:T(1024)S(1)}, f32[256,2048]{1,0:T(8,128)}, f32[256,2048]{1,0:T(8,128)}, f32[256,2048]{1,0:T(8,128)}) fusion(f32[256,2048]{1,0:T(8,128)S(1)} %get-tuple-element.547, f32[2048]{0:T(1024)S(1)} %bitcast.100, f32[256,2048]{1,0:T(8,128)} %get-tuple-element.526, pred[]{:T(512)S(6)} %compare.26, ...), kind=kOutput, calls=%fused_computation.27.clone.1 | convolution fusion | flops 1617033216 | bytes 16809984 | tf_op jit(solution)/shard_map/while/body/eval_jaxpr/dot_general | solution.py:58
  123.3 3.8 fusion.82
  127.1 9.1 %multiply_reduce_fusion.8 = (f32[2048]{0:T(1024)S(1)}, f32[256,2048]{1,0:T(8,128)}, f32[256,2048]{1,0:T(8,128)}, f32[256,2048]{1,0:T(8,128)}) fusion(f32[256,2048]{1,0:T(8,128)S(1)} %get-tuple-element.547, f32[2048]{0:T(1024)S(1)} %bitcast.100, f32[256,2048]{1,0:T(8,128)} %get-tuple-element.526, pred[]{:T(512)S(6)} %compare.26, ...), kind=kOutput, calls=%fused_computation.27.clone.1 | convolution fusion | flops 1617033216 | bytes 16809984 | tf_op jit(solution)/shard_map/while/body/eval_jaxpr/dot_general | solution.py:58
  140.7 3.8 fusion.82
  144.6 9.1 %multiply_reduce_fusion.8 = (f32[2048]{0:T(1024)S(1)}, f32[256,2048]{1,0:T(8,128)}, f32[256,2048]{1,0:T(8,128)}, f32[256,2048]{1,0:T(8,128)}) fusion(f32[256,2048]{1,0:T(8,128)S(1)} %get-tuple-element.547, f32[2048]{0:T(1024)S(1)} %bitcast.100, f32[256,2048]{1,0:T(8,128)} %get-tuple-element.526, pred[]{:T(512)S(6)} %compare.26, ...), kind=kOutput, calls=%fused_computation.27.clone.1 | convolution fusion | flops 1617033216 | bytes 16809984 | tf_op jit(solution)/shard_map/while/body/eval_jaxpr/dot_general | solution.py:58
  158.2 3.8 fusion.82
  162.0 9.1 %multiply_reduce_fusion.8 = (f32[2048]{0:T(1024)S(1)}, f32[256,2048]{1,0:T(8,128)}, f32[256,2048]{1,0:T(8,128)}, f32[256,2048]{1,0:T(8,128)}) fusion(f32[256,2048]{1,0:T(8,128)S(1)} %get-tuple-element.547, f32[2048]{0:T(1024)S(1)} %bitcast.100, f32[256,2048]{1,0:T(8,128)} %get-tuple-element.526, pred[]{:T(512)S(6)} %compare.26, ...), kind=kOutput, calls=%fused_computation.27.clone.1 | convolution fusion | flops 1617033216 | bytes 16809984 | tf_op jit(solution)/shard_map/while/body/eval_jaxpr/dot_general | solution.py:58
  175.6 3.8 fusion.82
  179.5 9.1 %multiply_reduce_fusion.8 = (f32[2048]{0:T(1024)S(1)}, f32[256,2048]{1,0:T(8,128)}, f32[256,2048]{1,0:T(8,128)}, f32[256,2048]{1,0:T(8,128)}) fusion(f32[256,2048]{1,0:T(8,128)S(1)} %get-tuple-element.547, f32[2048]{0:T(1024)S(1)} %bitcast.100, f32[256,2048]{1,0:T(8,128)} %get-tuple-element.526, pred[]{:T(512)S(6)} %compare.26, ...), kind=kOutput, calls=%fused_computation.27.clone.1 | convolution fusion | flops 1617033216 | bytes 16809984 | tf_op jit(solution)/shard_map/while/body/eval_jaxpr/dot_general | solution.py:58
  193.1 3.8 fusion.82
  196.9 9.1 %multiply_reduce_fusion.8 = (f32[2048]{0:T(1024)S(1)}, f32[256,2048]{1,0:T(8,128)}, f32[256,2048]{1,0:T(8,128)}, f32[256,2048]{1,0:T(8,128)}) fusion(f32[256,2048]{1,0:T(8,128)S(1)} %get-tuple-element.547, f32[2048]{0:T(1024)S(1)} %bitcast.100, f32[256,2048]{1,0:T(8,128)} %get-tuple-element.526, pred[]{:T(512)S(6)} %compare.26, ...), kind=kOutput, calls=%fused_computation.27.clone.1 | convolution fusion | flops 1617033216 | bytes 16809984 | tf_op jit(solution)/shard_map/while/body/eval_jaxpr/dot_general | solution.py:58
  210.5 3.8 fusion.82
  214.3 9.1 %multiply_reduce_fusion.8 = (f32[2048]{0:T(1024)S(1)}, f32[256,2048]{1,0:T(8,128)}, f32[256,2048]{1,0:T(8,128)}, f32[256,2048]{1,0:T(8,128)}) fusion(f32[256,2048]{1,0:T(8,128)S(1)} %get-tuple-element.547, f32[2048]{0:T(1024)S(1)} %bitcast.100, f32[256,2048]{1,0:T(8,128)} %get-tuple-element.526, pred[]{:T(512)S(6)} %compare.26, ...), kind=kOutput, calls=%fused_computation.27.clone.1 | convolution fusion | flops 1617033216 | bytes 16809984 | tf_op jit(solution)/shard_map/while/body/eval_jaxpr/dot_general | solution.py:58
  228.0 3.8 fusion.82
  231.8 9.1 %multiply_reduce_fusion.8 = (f32[2048]{0:T(1024)S(1)}, f32[256,2048]{1,0:T(8,128)}, f32[256,2048]{1,0:T(8,128)}, f32[256,2048]{1,0:T(8,128)}) fusion(f32[256,2048]{1,0:T(8,128)S(1)} %get-tuple-element.547, f32[2048]{0:T(1024)S(1)} %bitcast.100, f32[256,2048]{1,0:T(8,128)} %get-tuple-element.526, pred[]{:T(512)S(6)} %compare.26, ...), kind=kOutput, calls=%fused_computation.27.clone.1 | convolution fusion | flops 1617033216 | bytes 16809984 | tf_op jit(solution)/shard_map/while/body/eval_jaxpr/dot_general | solution.py:58
  245.4 3.8 fusion.82
  249.2 9.1 %multiply_reduce_fusion.8 = (f32[2048]{0:T(1024)S(1)}, f32[256,2048]{1,0:T(8,128)}, f32[256,2048]{1,0:T(8,128)}, f32[256,2048]{1,0:T(8,128)}) fusion(f32[256,2048]{1,0:T(8,128)S(1)} %get-tuple-element.547, f32[2048]{0:T(1024)S(1)} %bitcast.100, f32[256,2048]{1,0:T(8,128)} %get-tuple-element.526, pred[]{:T(512)S(6)} %compare.26, ...), kind=kOutput, calls=%fused_computation.27.clone.1 | convolution fusion | flops 1617033216 | bytes 16809984 | tf_op jit(solution)/shard_map/while/body/eval_jaxpr/dot_general | solution.py:58
  262.9 3.8 fusion.82
  266.7 9.1 %multiply_reduce_fusion.8 = (f32[2048]{0:T(1024)S(1)}, f32[256,2048]{1,0:T(8,128)}, f32[256,2048]{1,0:T(8,128)}, f32[256,2048]{1,0:T(8,128)}) fusion(f32[256,2048]{1,0:T(8,128)S(1)} %get-tuple-element.547, f32[2048]{0:T(1024)S(1)} %bitcast.100, f32[256,2048]{1,0:T(8,128)} %get-tuple-element.526, pred[]{:T(512)S(6)} %compare.26, ...), kind=kOutput, calls=%fused_computation.27.clone.1 | convolution fusion | flops 1617033216 | bytes 16809984 | tf_op jit(solution)/shard_map/while/body/eval_jaxpr/dot_general | solution.py:58
  280.3 3.8 fusion.82
  284.1 9.1 %multiply_reduce_fusion.8 = (f32[2048]{0:T(1024)S(1)}, f32[256,2048]{1,0:T(8,128)}, f32[256,2048]{1,0:T(8,128)}, f32[256,2048]{1,0:T(8,128)}) fusion(f32[256,2048]{1,0:T(8,128)S(1)} %get-tuple-element.547, f32[2048]{0:T(1024)S(1)} %bitcast.100, f32[256,2048]{1,0:T(8,128)} %get-tuple-element.526, pred[]{:T(512)S(6)} %compare.26, ...), kind=kOutput, calls=%fused_computation.27.clone.1 | convolution fusion | flops 1617033216 | bytes 16809984 | tf_op jit(solution)/shard_map/while/body/eval_jaxpr/dot_general | solution.py:58
  307.1 22.3 %fusion.20 = f32[1,256,2048]{2,0,1:T(1,128)} fusion(bf16[1,383,2048]{2,1,0:T(8,128)(2,1)S(1)} %maximum_bitcast_fusion.1, f32[128,1,2048]{2,0,1:T(8,128)S(1)} %bitcast.95), kind=kOutput, calls=%fused_computation.37 | convolution fusion | flops 805306368 | bytes 4714496 | tf_op jit(solution)/shard_map/conv_general_dilated | solution.py:14
  333.5 4.4 fusion.32
  341.7 6.3 collective-permute-start
  348.3 4.8 rev.12
  353.1 5.2 rev.13
  362.3 22.3 %fusion.26 = f32[1,256,2048]{2,0,1:T(1,128)} fusion(bf16[1,383,2048]{2,1,0:T(8,128)(2,1)S(1)} %maximum_bitcast_fusion, f32[128,1,2048]{2,0,1:T(8,128)S(1)} %bitcast.98), kind=kOutput, calls=%fused_computation.61 | convolution fusion | flops 805306368 | bytes 4714496 | tf_op jit(solution)/shard_map/conv_general_dilated | solution.py:14
  384.5 27.9 %fusion.24 = f32[1,128,2048]{2,0,1:T(1,128)S(1)} fusion(bf16[1,383,2048]{2,1,0:T(8,128)(2,1)S(1)} %maximum_bitcast_fusion, bf16[256,1,2048]{2,0,1:T(8,128)(2,1)S(1)} %bitcast.86), kind=kOutput, calls=%fused_computation.59 | convolution fusion | flops 134217728 | bytes 3665920 | tf_op jit(solution)/shard_map/conv_general_dilated | solution.py:14
  412.8 5.2 rev.15
  420.0 4.7 fusion.28
  430.4 40.0 %psum.28 = f32[7,2048]{1,0:T(8,128)S(1)} all-reduce(f32[7,2048]{1,0:T(8,128)S(1)} %rev.14), channel_id=1, replica_groups=mesh['ctx'=8,'ch'=4] {'ctx'}, use_global_device_ids=true, to_apply=%region_8.9 | all-reduce | flops 14336 | bytes 114688 | tf_op jit(solution)/shard_map/psum | solution.py:166
  473.8 138.3 %while.36 = (s32[]{:T(128)}, f32[256,2048]{1,0:T(8,128)}, f32[256,2048]{1,0:T(8,128)}, f32[16,2048]{1,0:T(8,128)S(1)}, f32[16,2048]{1,0:T(8,128)}, /*index=5*/f3...) while((s32[]{:T(128)}, f32[256,2048]{1,0:T(8,128)}, ...), condition=%wide.region_7.8_spmd.clone.clone, body=%wide.region_5.7_spmd.clone.clone.sunk | while | flops 5771778 | bytes 10646661 | solution.py:84
  477.0 5.3 multiply_add_fusion.3
  485.7 5.3 multiply_add_fusion.3
  494.3 5.3 multiply_add_fusion.3
  502.9 5.3 multiply_add_fusion.3
  511.6 5.3 multiply_add_fusion.3
  520.2 5.3 multiply_add_fusion.3
  528.9 5.3 multiply_add_fusion.3
  537.5 5.3 multiply_add_fusion.3
  546.1 5.3 multiply_add_fusion.3
  554.8 5.3 multiply_add_fusion.3
  563.4 5.3 multiply_add_fusion.3
  572.0 5.3 multiply_add_fusion.3
  580.7 5.3 multiply_add_fusion.3
  589.3 5.3 multiply_add_fusion.3
  598.0 5.3 multiply_add_fusion.3
  606.6 5.3 multiply_add_fusion.3
  613.4 4.9 fusion.30
  621.9 68.7 %all-reduce.3.cloned.1.call-done = (f32[128,2048]{1,0:T(8,128)}, f32[16,2048]{1,0:T(8,128)}) async-done(((f32[128,2048]{1,0:T(8,128)}, f32[16,2048]{1,0:T(8,128)}), (f32[128,2048]{1,0:T(8,128)}, f32[16,2048]{1,0:T(8,128)})) %all-reduce.3.cloned.1.call-update) | async-done | bytes 1179664 | tf_op jit(solution)/shard_map/psum | solution.py:166
  699.1 6.6 psum.31
  (374 shorter events, 178.5 us)
Async XLA Ops:
  7.2 2.2 copy-start.7
  7.2 463.8 %all-gather.5.cloned.1.call-start = ((), (), s32[]{:S(2)}) async-start(), calls=%async_computation | async-start | bytes 1179648 | tf_op jit(solution)/shard_map/all_gather | solution.py:137
  7.2 2.2 copy-start.14
  9.3 297.6 %copy-start.2 = (bf16[256,2048]{1,0:T(8,128)(2,1)}, bf16[256,2048]{1,0:T(8,128)(2,1)S(1)}, u32[]{:S(2)}) copy-start(bf16[256,2048]{1,0:T(8,128)(2,1)S(1)} %fusion.38) | copy-start | bytes 3145732
  9.4 3.7 copy-start.25
  9.4 3.7 copy-start.26
  9.8 1.0 copy-start.4
  11.7 286.0 %collective-permute-start.1 = (bf16[133,2048]{1,0:T(8,128)(2,1)}, bf16[133,2048]{1,0:T(8,128)(2,1)}, u32[]{:S(2)}, u32[]{:S(2)}) collective-permute-start(bf16[133,2048]{1,0:T(8,128)(2,1)} %pad_maximum_fusion.1), channel_id=1, source_target_pairs={{4,0},{8,4},{12,8},{16,12},{20,16},{24,20},{28,24},{5,1},{9,5},{13... | collective-permute-start | bytes 1634312 | tf_op jit(solution)/shard_map/ppermute | solution.py:10
  23.7 10.0 %slice-start = ((f32[256,2048]{1,0:T(8,128)}), f32[1,2048]{1,0:T(1,128)S(1)}, s32[]{:S(2)}) async-start(f32[256,2048]{1,0:T(8,128)} %fusion.82), calls=%async_computation.3 | async-start | bytes 16384 | tf_op jit(solution)/shard_map/while/body/eval_jaxpr/slice | solution.py:61
  39.9 11.2 %slice-start = ((f32[256,2048]{1,0:T(8,128)}), f32[1,2048]{1,0:T(1,128)S(1)}, s32[]{:S(2)}) async-start(f32[256,2048]{1,0:T(8,128)} %fusion.82), calls=%async_computation.3 | async-start | bytes 16384 | tf_op jit(solution)/shard_map/while/body/eval_jaxpr/slice | solution.py:61
  57.3 11.2 %slice-start = ((f32[256,2048]{1,0:T(8,128)}), f32[1,2048]{1,0:T(1,128)S(1)}, s32[]{:S(2)}) async-start(f32[256,2048]{1,0:T(8,128)} %fusion.82), calls=%async_computation.3 | async-start | bytes 16384 | tf_op jit(solution)/shard_map/while/body/eval_jaxpr/slice | solution.py:61
  74.8 11.2 %slice-start = ((f32[256,2048]{1,0:T(8,128)}), f32[1,2048]{1,0:T(1,128)S(1)}, s32[]{:S(2)}) async-start(f32[256,2048]{1,0:T(8,128)} %fusion.82), calls=%async_computation.3 | async-start | bytes 16384 | tf_op jit(solution)/shard_map/while/body/eval_jaxpr/slice | solution.py:61
  92.2 11.2 %slice-start = ((f32[256,2048]{1,0:T(8,128)}), f32[1,2048]{1,0:T(1,128)S(1)}, s32[]{:S(2)}) async-start(f32[256,2048]{1,0:T(8,128)} %fusion.82), calls=%async_computation.3 | async-start | bytes 16384 | tf_op jit(solution)/shard_map/while/body/eval_jaxpr/slice | solution.py:61
  109.7 11.2 %slice-start = ((f32[256,2048]{1,0:T(8,128)}), f32[1,2048]{1,0:T(1,128)S(1)}, s32[]{:S(2)}) async-start(f32[256,2048]{1,0:T(8,128)} %fusion.82), calls=%async_computation.3 | async-start | bytes 16384 | tf_op jit(solution)/shard_map/while/body/eval_jaxpr/slice | solution.py:61
  127.1 11.2 %slice-start = ((f32[256,2048]{1,0:T(8,128)}), f32[1,2048]{1,0:T(1,128)S(1)}, s32[]{:S(2)}) async-start(f32[256,2048]{1,0:T(8,128)} %fusion.82), calls=%async_computation.3 | async-start | bytes 16384 | tf_op jit(solution)/shard_map/while/body/eval_jaxpr/slice | solution.py:61
  144.6 11.2 %slice-start = ((f32[256,2048]{1,0:T(8,128)}), f32[1,2048]{1,0:T(1,128)S(1)}, s32[]{:S(2)}) async-start(f32[256,2048]{1,0:T(8,128)} %fusion.82), calls=%async_computation.3 | async-start | bytes 16384 | tf_op jit(solution)/shard_map/while/body/eval_jaxpr/slice | solution.py:61
  162.0 11.2 %slice-start = ((f32[256,2048]{1,0:T(8,128)}), f32[1,2048]{1,0:T(1,128)S(1)}, s32[]{:S(2)}) async-start(f32[256,2048]{1,0:T(8,128)} %fusion.82), calls=%async_computation.3 | async-start | bytes 16384 | tf_op jit(solution)/shard_map/while/body/eval_jaxpr/slice | solution.py:61
  179.4 11.2 %slice-start = ((f32[256,2048]{1,0:T(8,128)}), f32[1,2048]{1,0:T(1,128)S(1)}, s32[]{:S(2)}) async-start(f32[256,2048]{1,0:T(8,128)} %fusion.82), calls=%async_computation.3 | async-start | bytes 16384 | tf_op jit(solution)/shard_map/while/body/eval_jaxpr/slice | solution.py:61
  196.9 11.2 %slice-start = ((f32[256,2048]{1,0:T(8,128)}), f32[1,2048]{1,0:T(1,128)S(1)}, s32[]{:S(2)}) async-start(f32[256,2048]{1,0:T(8,128)} %fusion.82), calls=%async_computation.3 | async-start | bytes 16384 | tf_op jit(solution)/shard_map/while/body/eval_jaxpr/slice | solution.py:61
  214.3 11.2 %slice-start = ((f32[256,2048]{1,0:T(8,128)}), f32[1,2048]{1,0:T(1,128)S(1)}, s32[]{:S(2)}) async-start(f32[256,2048]{1,0:T(8,128)} %fusion.82), calls=%async_computation.3 | async-start | bytes 16384 | tf_op jit(solution)/shard_map/while/body/eval_jaxpr/slice | solution.py:61
  231.8 11.2 %slice-start = ((f32[256,2048]{1,0:T(8,128)}), f32[1,2048]{1,0:T(1,128)S(1)}, s32[]{:S(2)}) async-start(f32[256,2048]{1,0:T(8,128)} %fusion.82), calls=%async_computation.3 | async-start | bytes 16384 | tf_op jit(solution)/shard_map/while/body/eval_jaxpr/slice | solution.py:61
  249.2 11.2 %slice-start = ((f32[256,2048]{1,0:T(8,128)}), f32[1,2048]{1,0:T(1,128)S(1)}, s32[]{:S(2)}) async-start(f32[256,2048]{1,0:T(8,128)} %fusion.82), calls=%async_computation.3 | async-start | bytes 16384 | tf_op jit(solution)/shard_map/while/body/eval_jaxpr/slice | solution.py:61
  266.7 11.2 %slice-start = ((f32[256,2048]{1,0:T(8,128)}), f32[1,2048]{1,0:T(1,128)S(1)}, s32[]{:S(2)}) async-start(f32[256,2048]{1,0:T(8,128)} %fusion.82), calls=%async_computation.3 | async-start | bytes 16384 | tf_op jit(solution)/shard_map/while/body/eval_jaxpr/slice | solution.py:61
  284.1 11.2 %slice-start = ((f32[256,2048]{1,0:T(8,128)}), f32[1,2048]{1,0:T(1,128)S(1)}, s32[]{:S(2)}) async-start(f32[256,2048]{1,0:T(8,128)} %fusion.82), calls=%async_computation.3 | async-start | bytes 16384 | tf_op jit(solution)/shard_map/while/body/eval_jaxpr/slice | solution.py:61
  296.9 0.7 copy-start.24
  296.9 4.1 copy-start
  296.9 4.1 copy-start.21
  297.5 173.4 %all-gather.7.cloned.1.call-start = ((), (), s32[]{:S(2)}) async-start(), calls=%async_computation.1 | async-start | bytes 1179648 | tf_op jit(solution)/shard_map/all_gather | solution.py:138
  305.6 1.4 copy-start.17
  307.1 22.3 %copy-start.27 = (f32[7,2048]{1,0:T(8,128)S(1)}, f32[7,2048]{1,0:T(8,128)}, u32[]{:S(2)}) copy-start(f32[7,2048]{1,0:T(8,128)} %param.32) | copy-start | bytes 172036
  307.1 22.3 %copy-start.33 = (pred[8,33]{0,1:T(8,128)(4,1)S(1)}, pred[8,33]{0,1:T(8,128)(4,1)}, u32[]{:S(2)}) copy-start(pred[8,33]{0,1:T(8,128)(4,1)} %constant.79) | copy-start | bytes 796
  333.5 4.5 copy-start.13
  333.5 4.5 copy-start.15
  333.5 4.5 copy-start.16
  340.6 12.5 %copy-start.18 = (f32[128,2048]{1,0:T(8,128)S(1)}, f32[128,2048]{1,0:T(8,128)}, u32[]{:S(2)}) copy-start(f32[128,2048]{1,0:T(8,128)} %param.33) | copy-start | bytes 3145732
  341.7 19.1 %collective-permute-start = (bf16[133,2048]{1,0:T(8,128)(2,1)}, bf16[133,2048]{1,0:T(8,128)(2,1)}, u32[]{:S(2)}, u32[]{:S(2)}) collective-permute-start(bf16[133,2048]{1,0:T(8,128)(2,1)} %pad_maximum_fusion), channel_id=1, source_target_pairs={{0,4},{4,8},{8,12},{12,16},{16,20},{20,24},{24,28},{1,5},{5,9},{9,... | collective-permute-start | bytes 1634312 | tf_op jit(solution)/shard_map/ppermute | solution.py:10
  348.0 342.5 %all-reduce.3.cloned.1.call-start = ((), (), s32[]{:S(2)}) async-start(), calls=%async_computation.2 | async-start | bytes 2359296 | tf_op jit(solution)/shard_map/psum | solution.py:166
  359.4 2.9 copy-start.19
  362.3 22.3 %copy-start.3 = (bf16[256,2048]{1,0:T(8,128)(2,1)S(1)}, bf16[256,2048]{1,0:T(8,128)(2,1)}, u32[]{:S(2)}) copy-start(bf16[256,2048]{1,0:T(8,128)(2,1)} %copy-done.2) | copy-start | bytes 3145732
  418.7 1.2 copy-start.5
  425.1 1.1 copy-start.28
  425.2 1.1 copy-start.34
  428.6 42.3 %copy-start.20 = (f32[16,2048]{1,0:T(8,128)S(1)}, f32[16,2048]{1,0:T(8,128)}, u32[]{:S(2)}) copy-start(f32[16,2048]{1,0:T(8,128)} %get-tuple-element.349) | copy-start | bytes 393220
  428.7 42.3 %copy-start.29 = (f32[8]{0:T(128)S(1)}, f32[8]{0:T(128)}, u32[]{:S(2)}) copy-start(f32[8]{0:T(128)} %get-tuple-element.354) | copy-start | bytes 100
  428.7 42.3 %copy-start.30 = (f32[8]{0:T(128)S(1)}, f32[8]{0:T(128)}, u32[]{:S(2)}) copy-start(f32[8]{0:T(128)} %get-tuple-element.355) | copy-start | bytes 100
  428.7 42.3 %copy-start.31 = (pred[8]{0:T(512)(128)(4,1)S(1)}, pred[8]{0:T(512)(128)(4,1)}, u32[]{:S(2)}) copy-start(pred[8]{0:T(512)(128)(4,1)} %get-tuple-element.356) | copy-start | bytes 28
  428.7 42.3 %copy-start.32 = (pred[8]{0:T(512)(128)(4,1)S(1)}, pred[8]{0:T(512)(128)(4,1)}, u32[]{:S(2)}) copy-start(pred[8]{0:T(512)(128)(4,1)} %get-tuple-element.357) | copy-start | bytes 28
  430.4 43.4 %copy-start.1 = (f32[256,2048]{1,0:T(8,128)S(1)}, f32[256,2048]{1,0:T(8,128)}, u32[]{:S(2)}) copy-start(f32[256,2048]{1,0:T(8,128)} %copy-done) | copy-start | bytes 6291460
  473.8 138.4 %copy-start.22 = (f32[16,2048]{1,0:T(8,128)S(1)}, f32[16,2048]{1,0:T(8,128)}, u32[]{:S(2)}) copy-start(f32[16,2048]{1,0:T(8,128)} %copy-done.21) | copy-start | bytes 393220
  473.8 139.1 %copy-start.9 = (bf16[256,2048]{1,0:T(8,128)(2,1)S(1)}, bf16[256,2048]{1,0:T(8,128)(2,1)}, u32[]{:S(2)}) copy-start(bf16[256,2048]{1,0:T(8,128)(2,1)} %param.27) | copy-start | bytes 3145732
  612.1 1.3 copy-start.8
  613.4 4.9 copy-start.10
  613.4 4.9 copy-start.11
  618.3 77.9 %copy-start.12 = (bf16[256,2048]{1,0:T(8,128)(2,1)S(1)}, bf16[256,2048]{1,0:T(8,128)(2,1)}, u32[]{:S(2)}) copy-start(bf16[256,2048]{1,0:T(8,128)(2,1)} %param.31) | copy-start | bytes 3145732
  696.2 10.2 %copy-start.23 = (f32[16,2048]{1,0:T(8,128)S(1)}, f32[16,2048]{1,0:T(8,128)}, u32[]{:S(2)}) copy-start(f32[16,2048]{1,0:T(8,128)} %get-tuple-element.328) | copy-start | bytes 393220
  696.2 10.9 %copy-start.6 = (f32[128,2048]{1,0:T(8,128)S(1)}, f32[128,2048]{1,0:T(8,128)}, u32[]{:S(2)}) copy-start(f32[128,2048]{1,0:T(8,128)} %get-tuple-element.327) | copy-start | bytes 3145732
Sparse Core Ops, SparseCore 0:
  297.7 44.7 all-gather.4
  348.1 42.2 all-gather.6
  613.0 77.5 all-reduce.2
where the time goes:
time: 721 us; the launch traced here: 715 us
  matrix products  285 us (40%)
  other arithmetic  190 us (26%)
  local copies, waits for them, and re-layouts  97 us (13%)
  waiting for transfers between devices  70.2 us (10%)
  blocking collectives  46.6 us (6%)
  between operations  17 us (2%)
  starting transfers between devices  8.12 us (1%)
    dot_general x16, matrix products, one_mode(): jnp.dot(lower, grow * product_f, precision=lax.Precision.HIGHEST)  144 us
    add x16, other arithmetic, one_mode(): totals[1] + weight[None, :] * fade_back * leaving[None, :]  85.5 us
    conv_general_dilated x6, matrix products, depthwise(): lax.conv_general_dilated(signal[None], kernel[:, None, :], (1,), 'VALID',...  79.4 us
    psum x1, waiting for transfers between devices, body(): lax.psum((raw_short, raw_medium, raw_residue), 'ctx')  68.7 us
    dot_general x16, matrix products, one_mode(): jnp.dot(upper, shrink * signal_f, precision=lax.Precision.HIGHEST)  61.4 us
    psum x1, blocking collectives, body(): lax.psum((raw_short, raw_medium, raw_residue), 'ctx')  40 us
    dynamic_update_slice x64, local copies, waits for them, and re-layouts, long_local(): lax.scan(one_mode, (zeros, zeros), (decay_rates, weights, amplitudes))  33 us
    mul x16, other arithmetic, one_mode(): return (totals, amplitude * entering * jnp.sum(signal_f * fade_in, 0))  15 us
  transfers between devices with their start and end apart: 5, of which 2 were waited for; matrix products, arithmetic and copies ran while one was open for 58% of the time, Pallas kernels for 0%

commit v1 on v0

v1 whole, which is shorter than its diff:
```python
import functools

import jax
import jax.numpy as jnp
import numpy as np
from jax import lax
from jax.experimental import pallas as pl
from jax.experimental.pallas import tpu as pltpu
from jax.sharding import PartitionSpec as P

F32 = jnp.float32
BF16 = jnp.bfloat16
HALO = 16
MESH = pl.DeviceIdType.MESH


def from_behind(value, axis, steps):
    count = lax.axis_size(axis)
    first, last = (max(0, -steps), min(count, count - steps))
    return lax.ppermute(value, axis, [(source, source + steps) for source in range(first, last)])


def elementwise(first, second):
    return (first.astype(F32) * second.astype(F32)).astype(BF16)


def hi_lo(array):
    high = array.astype(BF16)
    low = (array - high.astype(F32)).astype(BF16)
    return high, low


def transform(size, points):
    turns = np.outer(2 * np.arange(size // 2) + 1, np.arange(points)) % (2 * size)
    angle = np.pi * turns / size
    return np.concatenate([np.cos(angle), np.sin(angle)], 0)


def np_hi_lo(matrix):
    matrix = np.asarray(matrix, np.float32)
    high = matrix.astype(jnp.bfloat16)
    low = (matrix - high.astype(np.float32)).astype(jnp.bfloat16)
    return np.stack([high, low])


def mul(first, second):
    return jnp.dot(first, second, preferred_element_type=F32)


def spectrum(matrix, data):
    return mul(matrix[0], data) + mul(matrix[1], data)


def wide(matrix, data):
    high, low = hi_lo(data)
    return mul(matrix[0], high) + (mul(matrix[0], low) + mul(matrix[1], high))


def convolved(first, second):
    half = first.shape[0] // 2
    fr, fs, sr, ss = first[:half], first[half:], second[:half], second[half:]
    return jnp.concatenate([fr * sr - fs * ss, fr * ss + fs * sr], 0)


def correlated(first, second):
    half = first.shape[0] // 2
    fr, fs, sr, ss = first[:half], first[half:], second[:half], second[half:]
    return jnp.concatenate([fr * sr + fs * ss, fs * sr - fr * ss], 0)


def ladder(rates):
    steps = lax.broadcasted_iota(jnp.int32, (1, 8, 1), 1).astype(F32)
    return jnp.exp(-rates[:, None, :] * steps), jnp.exp(-8.0 * rates)


def long_local_kernel(
    q_ref, k_ref, v_ref, g_ref, w_ref, d_ref, f_ref, i_ref, fl_ref, bl_ref, st_ref, h_scr, p_scr, s_scr
):
    length, width = q_ref.shape
    modes = d_ref.shape[0]
    tiles = length // 8
    product = elementwise(k_ref[...], v_ref[...])
    signal = elementwise(g_ref[...], q_ref[...])
    p_scr[...] = product.astype(F32)
    s_scr[...] = signal.astype(F32)
    for lane in range(0, width, 128):
        cols = slice(lane, lane + 128)
        rates = d_ref[:, cols]
        powers, step = ladder(rates)
        step = jnp.broadcast_to(step[:, None, :], (modes, 8, 128))

        def filter_step(a, state):
            h_scr[pl.ds(pl.multiple_of(a * 8, 8), 8), cols] = jnp.sum(state, 0)
            return state * step

        lax.fori_loop(0, tiles, filter_step, powers * w_ref[:, cols][:, None, :], unroll=4)
    ps = spectrum(f_ref, product)
    ss = spectrum(f_ref, signal)
    hs = wide(f_ref, h_scr[...])
    fl_ref[...] = wide(i_ref, convolved(ps, hs))
    bl_ref[...] = wide(i_ref, correlated(ss, hs))
    h_scr[...] = wide(i_ref, correlated(ss, ps))
    for lane in range(0, width, 128):
        cols = slice(lane, lane + 128)
        rates = d_ref[:, cols]
        powers, step = ladder(rates)
        step = jnp.broadcast_to(step[:, None, :], (modes, 8, 128))
        steps = lax.broadcasted_iota(jnp.int32, (1, 8, 1), 1).astype(F32)
        falling = jnp.exp(-rates[:, None, :] * (7.0 - steps))
        zeros = jnp.zeros((modes, 8, 128), F32)

        def end_step(a, state):
            return state * step + p_scr[pl.ds(pl.multiple_of(a * 8, 8), 8), cols][None]

        def start_step(a, states):
            at = pl.ds(pl.multiple_of((tiles - 1 - a) * 8, 8), 8)
            return (states[0] * step + s_scr[at, cols][None], states[1] * step + h_scr[at, cols][None])

        ends = lax.fori_loop(0, tiles, end_step, zeros, unroll=4)
        st_ref[0:modes, cols] = jnp.sum(ends * falling, 1)
        starts, lags = lax.fori_loop(0, tiles, start_step, (zeros, zeros), unroll=4)
        st_ref[modes : 2 * modes, cols] = jnp.sum(starts * powers, 1)
        st_ref[2 * modes : 3 * modes, cols] = jnp.sum(lags * powers, 1)


def explicit_kernel(
    qs, ks, vs, gs, qm, km, vm, gm, before, after, ts, tm, f_ref, i_ref,
    qs_o, ks_o, vs_o, qm_o, km_o, vm_o, raw_ref,
):
    length = qs.shape[0]
    taps = ts.shape[0]
    lags = tm.shape[0]
    product = elementwise(ks[...], vs[...]).astype(F32)
    signal = elementwise(gs[...], qs[...]).astype(F32)
    padded = jnp.concatenate([before[0:HALO].astype(F32), product], 0)
    trailing = jnp.concatenate([signal, after[0:HALO].astype(F32)], 0)
    forward = ts[0:1] * product
    backward = ts[0:1] * signal
    raw_ref[0:8, :] = jnp.zeros((8, raw_ref.shape[1]), F32)
    raw_ref[0:1, :] = jnp.sum(signal * product, 0, keepdims=True)
    for j in range(1, taps):
        shifted = padded[HALO - j : HALO - j + length]
        forward = forward + ts[j : j + 1] * shifted
        raw_ref[j : j + 1, :] = jnp.sum(signal * shifted, 0, keepdims=True)
        backward = backward + ts[j : j + 1] * trailing[j : j + length]
    qs_o[...] = (gs[...].astype(F32) * forward).astype(BF16)
    ks_o[...] = (backward * vs[...].astype(F32)).astype(BF16)
    vs_o[...] = (backward * ks[...].astype(F32)).astype(BF16)

    product = elementwise(km[...], vm[...])
    signal = elementwise(gm[...], qm[...])
    near = f_ref[:, :, 0:length]
    far = f_ref[:, :, length : length + lags]
    own = spectrum(near, product)
    ps = own - spectrum(far, before[HALO : HALO + lags])
    ss = spectrum(near, signal) + spectrum(far, after[HALO : HALO + lags])
    hs = wide(f_ref[:, :, 0:lags], tm[...])
    forward = wide(i_ref, convolved(ps, hs))
    backward = wide(i_ref, correlated(ss, hs))
    raw_ref[8 : 8 + lags, :] = wide(i_ref[:, 0:lags], correlated(ss, own))
    qm_o[...] = (gm[...].astype(F32) * forward).astype(BF16)
    km_o[...] = (backward * vm[...].astype(F32)).astype(BF16)
    vm_o[...] = (backward * km[...].astype(F32)).astype(BF16)


def long_final_kernel(k_ref, v_ref, g_ref, fl_ref, bl_ref, w_ref, d_ref, c_ref, qo, ko, vo, f_scr, b_scr):
    length, width = k_ref.shape
    modes = d_ref.shape[0]
    tiles = length // 8
    for lane in range(0, width, 128):
        cols = slice(lane, lane + 128)
        rates = d_ref[:, cols]
        powers, step = ladder(rates)
        step = jnp.broadcast_to(step[:, None, :], (modes, 8, 128))
        steps = lax.broadcasted_iota(jnp.int32, (1, 8, 1), 1).astype(F32)
        falling = jnp.exp(-rates[:, None, :] * (7.0 - steps))
        scale = w_ref[:, cols] * jnp.exp(-rates)
        into = (scale * c_ref[0:modes, cols])[:, None, :] * powers
        back = (scale * c_ref[modes : 2 * modes, cols])[:, None, :] * falling

        def one(a, states):
            f_scr[pl.ds(pl.multiple_of(a * 8, 8), 8), cols] = jnp.sum(states[0], 0)
            b_scr[pl.ds(pl.multiple_of((tiles - 1 - a) * 8, 8), 8), cols] = jnp.sum(states[1], 0)
            return (states[0] * step, states[1] * step)

        lax.fori_loop(0, tiles, one, (into, back), unroll=4)
    backward = bl_ref[...] + b_scr[...]
    qo[...] = (g_ref[...].astype(F32) * (fl_ref[...] + f_scr[...])).astype(BF16)
    ko[...] = (backward * v_ref[...].astype(F32)).astype(BF16)
    vo[...] = (backward * k_ref[...].astype(F32)).astype(BF16)


def exchange_kernel(
    count, groups, owners, length, entries,
    st, raw, rates, amp,
    short_o, medium_o, residue_o, carry_o,
    in_st, in_raw, out_c, out_s, in_c, in_s, own_sq, in_sq,
    st_send, st_recv, raw_send, raw_recv, c_send, c_recv, s_send, s_recv, q_send, q_recv,
):
    me = lax.axis_index("ctx")
    group = lax.axis_index("ch")
    modes = rates.shape[0]
    lags = medium_o.shape[0]
    taps = short_o.shape[0]
    width = rates.shape[1] // owners

    def guarded(condition, action):
        if owners == count:
            action()
        else:
            pl.when(condition)(action)

    barrier = pltpu.get_barrier_semaphore()
    for k in range(1, count):
        pl.semaphore_signal(barrier, inc=1, device_id={"ctx": lax.rem(me + k, count)}, device_id_type=MESH)
    for k in range(1, groups):
        pl.semaphore_signal(barrier, inc=1, device_id={"ch": lax.rem(group + k, groups)}, device_id_type=MESH)
    pl.semaphore_wait(barrier, count + groups - 2)

    def send(source, target, k, send_sem, recv_sem):
        return pltpu.make_async_remote_copy(
            src_ref=source, dst_ref=target, send_sem=send_sem.at[k], recv_sem=recv_sem.at[k],
            device_id={"ctx": lax.rem(me + k, count)}, device_id_type=MESH,
        )

    def chunk(owner):
        return pl.ds(pl.multiple_of(owner * width, 128), width)

    def gathered(k, slot):
        to = lax.rem(me + k, count)
        return (
            send(st.at[:, chunk(to)], in_st.at[slot], k, st_send, st_recv),
            send(raw.at[:, chunk(to)], in_raw.at[slot], k, raw_send, raw_recv),
        )

    def returned(k, slot, sums):
        to = lax.rem(me + k, count)
        if sums:
            return send(out_s, in_s.at[slot], k, s_send, s_recv)
        return send(out_c.at[to], in_c.at[slot], k, c_send, c_recv)

    for k in range(1, count):
        def start_one(k=k):
            for copy in gathered(k, me):
                copy.start()
        guarded(lax.rem(me + k, count) < owners, start_one)

    def own():
        in_st[me] = st[:, chunk(me)]
        in_raw[me] = raw[:, chunk(me)]
        for k in range(1, count):
            for copy in gathered(k, lax.rem(me + count - k, count)):
                copy.wait_recv()
        rate = rates[:, chunk(me)]
        fade = jnp.exp(-rate)
        over = jnp.exp(-float(length) * rate)
        carry = jnp.zeros(rate.shape, F32)
        residue = jnp.zeros(rate.shape, F32)
        for i in range(count):
            out_c[i, 0:modes] = carry
            starts = in_st[i, modes : 2 * modes]
            residue = residue + in_st[i, 2 * modes : 3 * modes] + carry * fade * starts
            carry = carry * over + in_st[i, 0:modes]
        carry = jnp.zeros(rate.shape, F32)
        for i in reversed(range(count)):
            out_c[i, modes : 2 * modes] = carry
            carry = carry * over + in_st[i, modes : 2 * modes]
        sums = in_raw[0]
        for i in range(1, count):
            sums = sums + in_raw[i]
        residue = residue * amp[:, chunk(me)]
        square = jnp.sum(jnp.sum(sums * sums, 0, keepdims=True), 1, keepdims=True) + jnp.sum(
            jnp.sum(residue * residue, 0, keepdims=True), 1, keepdims=True
        )
        square = jnp.broadcast_to(square, (8, width))
        for i in range(count):
            out_c[i, 2 * modes : 2 * modes + 8] = square
        out_s[...] = jnp.concatenate([sums, residue, jnp.zeros((8, width), F32)], 0).astype(BF16)
        for k in range(1, count):
            returned(k, me, False).start()
        for k in range(1, count):
            returned(k, me, True).start()
        in_c[me] = out_c[me]
        in_s[me] = out_s[...]

    guarded(me < owners, own)

    for k in range(1, count):
        source = lax.rem(me + count - k, count)
        def wait_carry(k=k, source=source):
            returned(k, source, False).wait_recv()
        guarded(source < owners, wait_carry)
    total = in_c[0, 2 * modes : 2 * modes + 8]
    for i in range(1, owners):
        total = total + in_c[i, 2 * modes : 2 * modes + 8]
    own_sq[...] = total
    in_sq[group] = total

    def shared(k, slot):
        return pltpu.make_async_remote_copy(
            src_ref=own_sq, dst_ref=in_sq.at[slot], send_sem=q_send.at[k], recv_sem=q_recv.at[k],
            device_id={"ch": lax.rem(group + k, groups)}, device_id_type=MESH,
        )

    for k in range(1, groups):
        shared(k, group).start()
    for i in range(owners):
        carry_o[:, i * width : (i + 1) * width] = in_c[i, 0 : 2 * modes]
    for k in range(1, count):
        source = lax.rem(me + count - k, count)
        def wait_sums(k=k, source=source):
            returned(k, source, True).wait_recv()
        guarded(source < owners, wait_sums)
    for k in range(1, groups):
        shared(k, lax.rem(group + groups - k, groups)).wait_recv()
    total = in_sq[0]
    for i in range(1, groups):
        total = total + in_sq[i]
    factor = (1.0 / jnp.sqrt(total / entries + 1e-06))[0:1]
    for i in range(owners):
        cols = slice(i * width, (i + 1) * width)
        block = in_s[i].astype(F32) * factor
        short_o[:, cols] = block[0:taps]
        medium_o[:, cols] = block[8 : 8 + lags]
        residue_o[:, cols] = block[8 + lags : 8 + lags + modes]
    for k in range(1, count):
        def wait_gather(k=k):
            for copy in gathered(k, me):
                copy.wait_send()
        guarded(lax.rem(me + k, count) < owners, wait_gather)
        def wait_return(k=k):
            returned(k, me, False).wait_send()
            returned(k, me, True).wait_send()
        guarded(me < owners, wait_return)
    for k in range(1, groups):
        shared(k, group).wait_send()


def exchange(st, raw, rates, amp, taps, lags, length):
    count, groups = lax.axis_size("ctx"), lax.axis_size("ch")
    modes, wide_c = rates.shape
    owners = min(count, wide_c // 128)
    width = wide_c // owners
    rows = raw.shape[0]
    entries = float((taps + lags + modes) * wide_c * groups)
    dma = pltpu.SemaphoreType.DMA
    vmem = pl.BlockSpec(memory_space=pltpu.VMEM)
    return pl.pallas_call(
        functools.partial(exchange_kernel, count, groups, owners, length, entries),
        out_shape=[
            jax.ShapeDtypeStruct((taps, wide_c), F32),
            jax.ShapeDtypeStruct((lags, wide_c), F32),
            jax.ShapeDtypeStruct((modes, wide_c), F32),
            jax.ShapeDtypeStruct((2 * modes, wide_c), F32),
        ],
        in_specs=[vmem] * 4,
        out_specs=[vmem] * 4,
        scratch_shapes=[
            pltpu.VMEM((count, 3 * modes, width), F32),
            pltpu.VMEM((count, rows, width), F32),
            pltpu.VMEM((count, 2 * modes + 8, width), F32),
            pltpu.VMEM((rows + modes + 8, width), BF16),
            pltpu.VMEM((owners, 2 * modes + 8, width), F32),
            pltpu.VMEM((owners, rows + modes + 8, width), BF16),
            pltpu.VMEM((8, width), F32),
            pltpu.VMEM((groups, 8, width), F32),
        ]
        + [dma((count,))] * 8
        + [dma((groups,))] * 2,
        compiler_params=pltpu.CompilerParams(
            collective_id=0, has_side_effects=True, vmem_limit_bytes=48 << 20
        ),
    )(st, raw, rates, amp)


def body(
    query_short, key_short, value_short, grad_short,
    query_medium, key_medium, value_medium, grad_medium,
    query_long, key_long, value_long, grad_long,
    taps_short, taps_medium, residues, decay_rates,
):
    length, channels = query_short.shape
    taps, lags, modes = taps_short.shape[0], taps_medium.shape[0], residues.shape[0]
    block = 256
    grid = (channels // block,)
    tails = jnp.concatenate(
        [
            elementwise(key_short[length - HALO :], value_short[length - HALO :]),
            elementwise(key_medium[length - lags :], value_medium[length - lags :]),
        ],
        0,
    )
    heads = jnp.concatenate(
        [
            elementwise(grad_short[:HALO], query_short[:HALO]),
            elementwise(grad_medium[:lags], query_medium[:lags]),
        ],
        0,
    )
    before = from_behind(tails, "ctx", 1)
    after = from_behind(heads, "ctx", -1)
    amplitudes = jnp.sqrt(-jnp.expm1(-2.0 * decay_rates))
    weights = amplitudes * residues

    def cols(rows):
        return pl.BlockSpec((rows, block), lambda i: (0, i))

    def const(shape):
        return pl.BlockSpec(shape, lambda i: (0,) * len(shape))

    def shape(rows, dtype):
        return jax.ShapeDtypeStruct((rows, channels), dtype)

    params = pltpu.CompilerParams(dimension_semantics=("arbitrary",), vmem_limit_bytes=48 << 20)
    full = 2 * length
    long_f = np_hi_lo(transform(full, length))
    long_i = np_hi_lo(transform(full, length).T * (2.0 / full))
    fl, bl, st = pl.pallas_call(
        long_local_kernel,
        grid=grid,
        in_specs=[cols(length)] * 4 + [cols(modes)] * 2 + [const(long_f.shape), const(long_i.shape)],
        out_specs=[cols(length), cols(length), cols(3 * modes)],
        out_shape=[shape(length, F32), shape(length, F32), shape(3 * modes, F32)],
        scratch_shapes=[pltpu.VMEM((length, block), F32)] * 3,
        compiler_params=params,
        cost_estimate=pl.CostEstimate(flops=20_000_000_000, bytes_accessed=8_000_000, transcendentals=0),
    )(query_long, key_long, value_long, grad_long, weights, decay_rates, jnp.asarray(long_f), jnp.asarray(long_i))

    part = length + lags
    part_f = np_hi_lo(transform(part, part))
    part_i = np_hi_lo(transform(part, length).T * (2.0 / part))
    outs = pl.pallas_call(
        explicit_kernel,
        grid=grid,
        in_specs=[cols(length)] * 8
        + [cols(HALO + lags)] * 2
        + [cols(taps), cols(lags), const(part_f.shape), const(part_i.shape)],
        out_specs=[cols(length)] * 6 + [cols(8 + lags)],
        out_shape=[shape(length, BF16)] * 6 + [shape(8 + lags, F32)],
        compiler_params=params,
        cost_estimate=pl.CostEstimate(flops=20_000_000_000, bytes_accessed=16_000_000, transcendentals=0),
    )(
        query_short, key_short, value_short, grad_short,
        query_medium, key_medium, value_medium, grad_medium,
        before, after, taps_short, taps_medium, jnp.asarray(part_f), jnp.asarray(part_i),
    )
    short_g, medium_g, residue_g, carries = exchange(
        st, outs[6], decay_rates, amplitudes, taps, lags, length
    )
    long_outs = pl.pallas_call(
        long_final_kernel,
        grid=grid,
        in_specs=[cols(length)] * 5 + [cols(modes)] * 2 + [cols(2 * modes)],
        out_specs=[cols(length)] * 3,
        out_shape=[shape(length, BF16)] * 3,
        scratch_shapes=[pltpu.VMEM((length, block), F32)] * 2,
        compiler_params=params,
        cost_estimate=pl.CostEstimate(flops=1_000_000_000, bytes_accessed=10_000_000, transcendentals=0),
    )(key_long, value_long, grad_long, fl, bl, weights, decay_rates, carries)
    return (*outs[:6], *long_outs, short_g, medium_g, residue_g)


def solution(mesh):
    tokens, filters = P("ctx", "ch"), P(None, "ch")
    return jax.shard_map(
        body,
        mesh=mesh,
        in_specs=(tokens,) * 12 + (filters,) * 4,
        out_specs=(tokens,) * 9 + (filters,) * 3,
        check_vma=False,
    )
```

time: 721 us -> 146 us (0.20)
  matrix products: 285 us -> 0 us
  other arithmetic: 190 us -> 5.82 us
  Pallas kernels: 0 us -> 129 us
  local copies, waits for them, and re-layouts: 97 us -> 3.59 us
  waiting for transfers between devices: 70.2 us -> 0.01 us
  blocking collectives: 46.6 us -> 0 us
  between operations: 17 us -> 0.93 us
    dot_general x32 -> x0, matrix products: 206 us -> none  [the longest x16 144 us: one_mode(): jnp.dot(lower, grow * product_f, precision=lax.Precision.HIGHEST)]
    pallas_call x0 -> x4, Pallas kernels: none -> 129 us  [the longest x1 63.6 us: exchange(): pl.pallas_call(functools.partial(exchange_kernel, count, groups, owners,...]
    add x33 -> x0, other arithmetic: 86.4 us -> none  [the longest x16 85.5 us: one_mode(): totals[1] + weight[None, :] * fade_back * leaving[None, :]]
    conv_general_dilated x6 -> x0, matrix products: 79.4 us -> none  [depthwise(): lax.conv_general_dilated(signal[None], kernel[:, None, :], (1,), 'VALID',...]
    psum x1 -> x0, waiting for transfers between devices: 68.7 us -> none  [body(): lax.psum((raw_short, raw_medium, raw_residue), 'ctx')]
    psum x2 -> x0, blocking collectives: 46.6 us -> none  [the longest x1 40 us: body(): lax.psum((raw_short, raw_medium, raw_residue), 'ctx')]
    dynamic_update_slice x64 -> x0, local copies, waits for them, and re-layouts: 33 us -> none  [long_local(): lax.scan(one_mode, (zeros, zeros), (decay_rates, weights, amplitudes))]
    mul x35 -> x0, other arithmetic: 31 us -> none  [the longest x16 15 us: one_mode(): return (totals, amplitude * entering * jnp.sum(signal_f * fade_in, 0))]
  transfers between devices with their start and end apart: 5 -> 2, of which waited for: 2 -> 0; matrix products, arithmetic and copies ran while one was open for 58% -> 2% of each run, Pallas kernels for 0% -> 21%
where the time goes in v1:
time: 146 us
  Pallas kernels  129 us (88%)
  starting transfers between devices  6.46 us (4%)
  other arithmetic  5.82 us (4%)
  local copies, waits for them, and re-layouts  3.59 us (2%)
    pallas_call x1, Pallas kernels, exchange(): pl.pallas_call(functools.partial(exchange_kernel, count, groups, owners,...  63.6 us
    pallas_call x1, Pallas kernels, body(): pl.pallas_call(long_local_kernel, grid=grid, in_specs=[cols(length)] * 4...  31 us
    pallas_call x1, Pallas kernels, body(): pl.pallas_call(explicit_kernel, grid=grid, in_specs=[cols(length)] * 8 +...  24.4 us
    pallas_call x1, Pallas kernels, body(): pl.pallas_call(long_final_kernel, grid=grid, in_specs=[cols(length)] * 5...  9.89 us
    ppermute x2, starting transfers between devices, from_behind(): lax.ppermute(value, axis, [(source, source + steps) for source in range(f...  6.46 us
    convert_element_type x4, other arithmetic, elementwise(): return (first.astype(F32) * second.astype(F32)).astype(BF16)  4.73 us
    unnamed x33, local copies, waits for them, and re-layouts  3.59 us
  transfers between devices with their start and end apart: 2, of which 0 were waited for; matrix products, arithmetic and copies ran while one was open for 2% of the time, Pallas kernels for 21%

profile of v1, /device:TPU:0, one launch (start us, length us, event | category | flops | bytes accessed | tf_op | source)
XLA Modules:
  0.0 145.6 jit_solution(10196419722648408065)
XLA Ops:
  0.6 0.0 copy-start.13
  0.7 0.9 multiply_convert_fusion.3
  1.6 0.0 copy-start.6
  1.6 0.0 copy-start.12
  1.6 1.4 multiply_convert_fusion.1
  3.1 0.0 copy-start.9
  3.1 5.0 %collective-permute-start = (bf16[144,2048]{1,0:T(8,128)(2,1)S(1)}, bf16[144,2048]{1,0:T(8,128)(2,1)S(1)}, u32[]{:S(2)}, u32[]{:S(2)}) collective-permute-start(bf16[144,2048]{1,0:T(8,128)(2,1)S(1)} %pad_maximum_fusion), channel_id=1, source_target_pairs={{0,4},{4,8},{8,12},{12,16},{16,20},{20,24},{24,28},{1,5},{5,9},{9,... | collective-permute-start | bytes 1769480 | tf_op jit(solution)/shard_map/ppermute | solution.py:20
  8.2 0.0 copy-done.6
  8.2 0.9 multiply_convert_fusion.2
  9.1 0.0 copy-start.1
  9.1 0.0 copy-start.4
  9.1 0.0 copy-start.5
  9.1 1.5 %multiply_convert_fusion = bf16[128,2048]{1,0:T(8,128)(2,1)S(1)} fusion(bf16[256,2048]{1,0:T(8,128)(2,1)} %qm.1, bf16[256,2048]{1,0:T(8,128)(2,1)} %gm.1), kind=kLoop, calls=%fused_computation | loop fusion | flops 1048576 | bytes 1572864 | tf_op jit(solution)/shard_map/convert_element_type | solution.py:24
  10.6 0.0 copy-start.3
  10.7 1.4 collective-permute-start.1
  12.1 0.0 copy-done.1
  12.1 1.0 negate_sqrt_fusion
  13.1 0.0 copy-done.13
  13.1 0.0 copy-done.12
  13.1 0.0 copy-done.9
  13.1 0.0 copy-done.4
  13.1 0.0 copy-done.5
  13.1 0.0 copy-done.3
  13.2 0.0 copy-start.7
  13.2 0.0 copy-start.8
  13.2 0.0 copy-start.10
  13.2 0.0 copy-start.11
  13.2 0.0 copy-start.14
  13.2 31.0 %shard_map.284 = (f32[256,2048]{1,0:T(8,128)}, f32[256,2048]{1,0:T(8,128)}, f32[48,2048]{1,0:T(8,128)S(1)}) custom-call(bf16[256,2048]{1,0:T(8,128)(2,1)S(1)} %copy-done.9, bf16[256,2048]{1,0:T(8,128)(2,1)S(1)} %copy-done.3, bf16[256,2048]{1,0:T(8,128)(2,1)S(1)} %copy-done.4, bf16[256,2048]{1,0:T(8,128)(2,1)S(1)} %copy-done.5, ...), custom_call_target="tpu_custom_call" | custom-call | flops 20000000000 | bytes 8000000 | tf_op jit(solution)/shard_map/pallas_call | solution.py:418
  44.2 0.0 collective-permute-done.before
  44.2 0.0 collective-permute-done.1.after
  44.2 0.0 copy-done.7
  44.2 0.0 copy-done.8
  44.2 0.0 copy-done.10
  44.2 0.0 copy-done.11
  44.2 0.0 copy-done.14
  44.2 0.0 copy-start
  44.2 24.4 %shard_map.283 = (bf16[256,2048]{1,0:T(8,128)(2,1)}, bf16[256,2048]{1,0:T(8,128)(2,1)}, bf16[256,2048]{1,0:T(8,128)(2,1)}, bf16[256,2048]{1,0:T(8,128)(2,1)}, bf...) custom-call(bf16[256,2048]{1,0:T(8,128)(2,1)S(1)} %copy-done.6, ...), custom_call_target="tpu_custom_call" | custom-call | flops 20000000000 | bytes 16000000 | tf_op jit(solution)/shard_map/pallas_call | solution.py:432
  68.6 0.0 copy-start.2
  68.6 1.2 copy-done.2
  69.8 63.6 %shard_map.285 = (f32[7,2048]{1,0:T(8,128)S(1)}, f32[128,2048]{1,0:T(8,128)S(1)}, f32[16,2048]{1,0:T(8,128)S(1)}, f32[32,2048]{1,0:T(8,128)S(1)}) custom-call(f32[48,2048]{1,0:T(8,128)S(1)} %get-tuple-element.37.st, f32[136,2048]{1,0:T(8,128)S(1)} %copy-done.2, f32[16,2048]{1,0:T(8,128)S(1)} %copy-done.1, f32[16,2048]{1,0:T(8,128)S(1)} %get-tuple-element.46.amp), custom_call_target="tpu_custom_call" | custom-call | tf_op jit(solution)/shard_map/pallas_call | solution.py:348
  133.4 0.0 copy-done
  133.4 9.9 %shard_map.286 = (bf16[256,2048]{1,0:T(8,128)(2,1)}, bf16[256,2048]{1,0:T(8,128)(2,1)}, bf16[256,2048]{1,0:T(8,128)(2,1)}) custom-call(bf16[256,2048]{1,0:T(8,128)(2,1)S(1)} %copy-done.3, bf16[256,2048]{1,0:T(8,128)(2,1)S(1)} %copy-done.4, bf16[256,2048]{1,0:T(8,128)(2,1)S(1)} %copy-done.5, f32[256,2048]{1,0:T(8,128)S(1)} %copy-done, ...), custom_call_target="tpu_custom_call" | custom-call | flops 1000000000 | bytes 10000000 | tf_op jit(solution)/shard_map/pallas_call | solution.py:450
  143.3 0.6 copy.35
  143.9 1.0 copy.36
  144.9 0.7 copy.37
  (2 shorter events, 0.1 us)
Async XLA Ops:
  0.6 12.5 %copy-start.13 = (bf16[2,512,256]{2,1,0:T(8,128)(2,1)S(1)}, bf16[2,512,256]{2,1,0:T(8,128)(2,1)}, u32[]{:S(2)}) copy-start(bf16[2,512,256]{2,1,0:T(8,128)(2,1)} %constant.10.clone.f_ref) | copy-start | bytes 1572868
  1.6 6.6 %copy-start.6 = (bf16[256,2048]{1,0:T(8,128)(2,1)S(1)}, bf16[256,2048]{1,0:T(8,128)(2,1)}, u32[]{:S(2)}) copy-start(bf16[256,2048]{1,0:T(8,128)(2,1)} %qs.1) | copy-start | bytes 3145732
  1.6 11.5 %copy-start.12 = (bf16[2,256,512]{2,1,0:T(8,128)(2,1)S(1)}, bf16[2,256,512]{2,1,0:T(8,128)(2,1)}, u32[]{:S(2)}) copy-start(bf16[2,256,512]{2,1,0:T(8,128)(2,1)} %constant.11.clone.i_ref) | copy-start | bytes 1572868
  3.1 10.0 %copy-start.9 = (bf16[256,2048]{1,0:T(8,128)(2,1)S(1)}, bf16[256,2048]{1,0:T(8,128)(2,1)}, u32[]{:S(2)}) copy-start(bf16[256,2048]{1,0:T(8,128)(2,1)} %q_ref.1) | copy-start | bytes 3145732
  3.1 41.0 %collective-permute-start = (bf16[144,2048]{1,0:T(8,128)(2,1)S(1)}, bf16[144,2048]{1,0:T(8,128)(2,1)S(1)}, u32[]{:S(2)}, u32[]{:S(2)}) collective-permute-start(bf16[144,2048]{1,0:T(8,128)(2,1)S(1)} %pad_maximum_fusion), channel_id=1, source_target_pairs={{0,4},{4,8},{8,12},{12,16},{16,20},{20,24},{24,28},{1,5},{5,9},{9,... | collective-permute-start | bytes 1769480 | tf_op jit(solution)/shard_map/ppermute | solution.py:20
  9.1 3.0 %copy-start.1 = (f32[16,2048]{1,0:T(8,128)S(1)}, f32[16,2048]{1,0:T(8,128)}, u32[]{:S(2)}) copy-start(f32[16,2048]{1,0:T(8,128)} %d_ref.3) | copy-start | bytes 393220
  9.1 4.0 %copy-start.4 = (bf16[256,2048]{1,0:T(8,128)(2,1)S(1)}, bf16[256,2048]{1,0:T(8,128)(2,1)}, u32[]{:S(2)}) copy-start(bf16[256,2048]{1,0:T(8,128)(2,1)} %v_ref.3) | copy-start | bytes 3145732
  9.1 4.0 %copy-start.5 = (bf16[256,2048]{1,0:T(8,128)(2,1)S(1)}, bf16[256,2048]{1,0:T(8,128)(2,1)}, u32[]{:S(2)}) copy-start(bf16[256,2048]{1,0:T(8,128)(2,1)} %g_ref.3) | copy-start | bytes 3145732
  10.6 2.6 %copy-start.3 = (bf16[256,2048]{1,0:T(8,128)(2,1)S(1)}, bf16[256,2048]{1,0:T(8,128)(2,1)}, u32[]{:S(2)}) copy-start(bf16[256,2048]{1,0:T(8,128)(2,1)} %k_ref.3) | copy-start | bytes 3145732
  10.7 33.5 %collective-permute-start.1 = (bf16[144,2048]{1,0:T(8,128)(2,1)S(1)}, bf16[144,2048]{1,0:T(8,128)(2,1)S(1)}, u32[]{:S(2)}, u32[]{:S(2)}) collective-permute-start(bf16[144,2048]{1,0:T(8,128)(2,1)S(1)} %pad_maximum_fusion.1), channel_id=1, source_target_pairs={{4,0},{8,4},{12,8},{16,12},{20,16},{24,20},{28,24},{5,1},{9,5},{13... | collective-permute-start | bytes 1769480 | tf_op jit(solution)/shard_map/ppermute | solution.py:20
  13.2 31.0 %copy-start.7 = (bf16[256,2048]{1,0:T(8,128)(2,1)S(1)}, bf16[256,2048]{1,0:T(8,128)(2,1)}, u32[]{:S(2)}) copy-start(bf16[256,2048]{1,0:T(8,128)(2,1)} %ks.1) | copy-start | bytes 3145732
  13.2 31.0 %copy-start.8 = (bf16[256,2048]{1,0:T(8,128)(2,1)S(1)}, bf16[256,2048]{1,0:T(8,128)(2,1)}, u32[]{:S(2)}) copy-start(bf16[256,2048]{1,0:T(8,128)(2,1)} %vs.1) | copy-start | bytes 3145732
  13.2 31.0 %copy-start.10 = (f32[7,2048]{1,0:T(8,128)S(1)}, f32[7,2048]{1,0:T(8,128)}, u32[]{:S(2)}) copy-start(f32[7,2048]{1,0:T(8,128)} %ts.1) | copy-start | bytes 172036
  13.2 31.0 %copy-start.11 = (bf16[2,384,384]{2,1,0:T(8,128)(2,1)S(1)}, bf16[2,384,384]{2,1,0:T(8,128)(2,1)}, u32[]{:S(2)}) copy-start(bf16[2,384,384]{2,1,0:T(8,128)(2,1)} %constant.12.clone.f_ref) | copy-start | bytes 1769476
  13.2 31.0 %copy-start.14 = (bf16[2,256,384]{2,1,0:T(8,128)(2,1)S(1)}, bf16[2,256,384]{2,1,0:T(8,128)(2,1)}, u32[]{:S(2)}) copy-start(bf16[2,256,384]{2,1,0:T(8,128)(2,1)} %constant.13.clone.i_ref) | copy-start | bytes 1179652
  44.2 89.2 %copy-start = (f32[256,2048]{1,0:T(8,128)S(1)}, f32[256,2048]{1,0:T(8,128)}, u32[]{:S(2)}) copy-start(f32[256,2048]{1,0:T(8,128)} %get-tuple-element.35.fl_ref) | copy-start | bytes 6291460
  68.6 1.2 copy-start.2

commit v2 on v1

--- a/solution.py
+++ b/solution.py
@@ -54,6 +54,11 @@
 def wide(matrix, data):
     high, low = hi_lo(data)
     return mul(matrix[0], high) + (mul(matrix[0], low) + mul(matrix[1], high))
+
+
+def inverse(matrix, data):
+    high, low = hi_lo(data)
+    return mul(matrix, high) + mul(matrix, low)
 
 
 def convolved(first, second):
@@ -97,9 +102,9 @@
     ps = spectrum(f_ref, product)
     ss = spectrum(f_ref, signal)
     hs = wide(f_ref, h_scr[...])
-    fl_ref[...] = wide(i_ref, convolved(ps, hs))
-    bl_ref[...] = wide(i_ref, correlated(ss, hs))
-    h_scr[...] = wide(i_ref, correlated(ss, ps))
+    fl_ref[...] = inverse(i_ref[...], convolved(ps, hs))
+    bl_ref[...] = inverse(i_ref[...], correlated(ss, hs))
+    h_scr[...] = inverse(i_ref[...], correlated(ss, ps))
     for lane in range(0, width, 128):
         cols = slice(lane, lane + 128)
         rates = d_ref[:, cols]
@@ -136,13 +141,14 @@
     trailing = jnp.concatenate([signal, after[0:HALO].astype(F32)], 0)
     forward = ts[0:1] * product
     backward = ts[0:1] * signal
-    raw_ref[0:8, :] = jnp.zeros((8, raw_ref.shape[1]), F32)
-    raw_ref[0:1, :] = jnp.sum(signal * product, 0, keepdims=True)
+    sums = [jnp.sum(signal * product, 0, keepdims=True)]
     for j in range(1, taps):
         shifted = padded[HALO - j : HALO - j + length]
         forward = forward + ts[j : j + 1] * shifted
-        raw_ref[j : j + 1, :] = jnp.sum(signal * shifted, 0, keepdims=True)
+        sums.append(jnp.sum(signal * shifted, 0, keepdims=True))
         backward = backward + ts[j : j + 1] * trailing[j : j + length]
+    sums.append(jnp.zeros((HALO - taps, sums[0].shape[1]), F32))
+    raw_ref[0:HALO, :] = jnp.concatenate(sums, 0).astype(BF16)
     qs_o[...] = (gs[...].astype(F32) * forward).astype(BF16)
     ks_o[...] = (backward * vs[...].astype(F32)).astype(BF16)
     vs_o[...] = (backward * ks[...].astype(F32)).astype(BF16)
@@ -155,15 +161,17 @@
     ps = own - spectrum(far, before[HALO : HALO + lags])
     ss = spectrum(near, signal) + spectrum(far, after[HALO : HALO + lags])
     hs = wide(f_ref[:, :, 0:lags], tm[...])
-    forward = wide(i_ref, convolved(ps, hs))
-    backward = wide(i_ref, correlated(ss, hs))
-    raw_ref[8 : 8 + lags, :] = wide(i_ref[:, 0:lags], correlated(ss, own))
+    forward = inverse(i_ref[...], convolved(ps, hs))
+    backward = inverse(i_ref[...], correlated(ss, hs))
+    raw_ref[HALO : HALO + lags, :] = inverse(i_ref[0:lags], correlated(ss, own)).astype(BF16)
     qm_o[...] = (gm[...].astype(F32) * forward).astype(BF16)
     km_o[...] = (backward * vm[...].astype(F32)).astype(BF16)
     vm_o[...] = (backward * km[...].astype(F32)).astype(BF16)
 
 
-def long_final_kernel(k_ref, v_ref, g_ref, fl_ref, bl_ref, w_ref, d_ref, c_ref, qo, ko, vo, f_scr, b_scr):
+def long_final_kernel(
+    early, k_ref, v_ref, g_ref, fl_a, fl_b, bl_a, bl_b, w_ref, d_ref, c_ref, qo, ko, vo, f_scr, b_scr
+):
     length, width = k_ref.shape
     modes = d_ref.shape[0]
     tiles = length // 8
@@ -184,31 +192,117 @@
             return (states[0] * step, states[1] * step)
 
         lax.fori_loop(0, tiles, one, (into, back), unroll=4)
-    backward = bl_ref[...] + b_scr[...]
-    qo[...] = (g_ref[...].astype(F32) * (fl_ref[...] + f_scr[...])).astype(BF16)
-    ko[...] = (backward * v_ref[...].astype(F32)).astype(BF16)
-    vo[...] = (backward * k_ref[...].astype(F32)).astype(BF16)
+
+    def finish(fl_ref, bl_ref):
+        backward = bl_ref[...] + b_scr[...]
+        qo[...] = (g_ref[...].astype(F32) * (fl_ref[...] + f_scr[...])).astype(BF16)
+        ko[...] = (backward * v_ref[...].astype(F32)).astype(BF16)
+        vo[...] = (backward * k_ref[...].astype(F32)).astype(BF16)
+
+    first = pl.program_id(0) < early
+    pl.when(first)(lambda: finish(fl_a, bl_a))
+    pl.when(jnp.logical_not(first))(lambda: finish(fl_b, bl_b))
+
+
+def guarded(always, condition, action):
+    if always:
+        action()
+    else:
+        pl.when(condition)(action)
+
+
+def chunk(owner, width):
+    return pl.ds(pl.multiple_of(owner * width, 128), width)
+
+
+def peer_copy(source, target, k, send_sem, recv_sem, count, me):
+    return pltpu.make_async_remote_copy(
+        src_ref=source, dst_ref=target, send_sem=send_sem.at[k], recv_sem=recv_sem.at[k],
+        device_id={"ctx": lax.rem(me + k, count)}, device_id_type=MESH,
+    )
+
+
+def long_sums_kernel(
+    count, owners,
+    q_ref, k_ref, v_ref, g_ref, w_ref, d_ref, f_ref, i_ref, raw,
+    fl_ref, bl_ref, st_ref, sums_o, square_o,
+    h_scr, p_scr, s_scr, in_raw, total_s, in_s,
+    own_sem, raw_send, raw_recv, s_send, s_recv,
+):
+    me = lax.axis_index("ctx")
+    step, steps = pl.program_id(0), pl.num_programs(0)
+    width = in_raw.shape[2]
+    every = owners == count
+
+    def gathered(k, slot):
+        source = raw.at[:, chunk(lax.rem(me + k, count), width)]
+        return peer_copy(source, in_raw.at[slot], k, raw_send, raw_recv, count, me)
+
+    def returned(k, slot):
+        return peer_copy(total_s, in_s.at[slot], k, s_send, s_recv, count, me)
+
+    def kept():
+        return pltpu.make_async_copy(raw.at[:, chunk(me, width)], in_raw.at[me], own_sem)
+
+    @pl.when(step == 0)
+    def _():
+        barrier = pltpu.get_barrier_semaphore()
+        for k in range(1, count):
+            pl.semaphore_signal(barrier, inc=1, device_id={"ctx": lax.rem(me + k, count)}, device_id_type=MESH)
+        pl.semaphore_wait(barrier, count - 1)
+        for k in range(1, count):
+            guarded(every, lax.rem(me + k, count) < owners, lambda k=k: gathered(k, me).start())
+        guarded(every, me < owners, lambda: kept().start())
+
+    @pl.when(step == steps // 2)
+    def _():
+        def own():
+            kept().wait()
+            for k in range(1, count):
+                gathered(k, lax.rem(me + count - k, count)).wait_recv()
+            sums = in_raw[0].astype(F32)
+            for i in range(1, count):
+                sums = sums + in_raw[i].astype(F32)
+            square = jnp.sum(jnp.sum(sums * sums, 0, keepdims=True), 1, keepdims=True)
+            square_o[...] = jnp.broadcast_to(square, square_o.shape)
+            total_s[...] = sums.astype(BF16)
+            for k in range(1, count):
+                returned(k, me).start()
+            in_s[me] = total_s[...]
+
+        if not every:
+            square_o[...] = jnp.zeros(square_o.shape, F32)
+        guarded(every, me < owners, own)
+
+    long_local_kernel(
+        q_ref, k_ref, v_ref, g_ref, w_ref, d_ref, f_ref, i_ref, fl_ref, bl_ref, st_ref, h_scr, p_scr, s_scr
+    )
+
+    @pl.when(step == steps - 1)
+    def _():
+        for k in range(1, count):
+            source = lax.rem(me + count - k, count)
+            guarded(every, source < owners, lambda k=k, source=source: returned(k, source).wait_recv())
+        sums_o[...] = in_s[...]
+        for k in range(1, count):
+            guarded(every, lax.rem(me + k, count) < owners, lambda k=k: gathered(k, me).wait_send())
+            guarded(every, me < owners, lambda k=k: returned(k, me).wait_send())
 
 
 def exchange_kernel(
     count, groups, owners, length, entries,
-    st, raw, rates, amp,
+    st, sums, square, rates, amp,
     short_o, medium_o, residue_o, carry_o,
-    in_st, in_raw, out_c, out_s, in_c, in_s, own_sq, in_sq,
-    st_send, st_recv, raw_send, raw_recv, c_send, c_recv, s_send, s_recv, q_send, q_recv,
+    in_st, out_c, in_c, own_sq, in_sq,
+    st_send, st_recv, c_send, c_recv, q_send, q_recv,
 ):
     me = lax.axis_index("ctx")
     group = lax.axis_index("ch")
     modes = rates.shape[0]
     lags = medium_o.shape[0]
     taps = short_o.shape[0]
-    width = rates.shape[1] // owners
-
-    def guarded(condition, action):
-        if owners == count:
-            action()
-        else:
-            pl.when(condition)(action)
+    width = in_st.shape[2]
+    every = owners == count
 
     barrier = pltpu.get_barrier_semaphore()
     for k in range(1, count):
@@ -217,43 +311,23 @@
         pl.semaphore_signal(barrier, inc=1, device_id={"ch": lax.rem(group + k, groups)}, device_id_type=MESH)
     pl.semaphore_wait(barrier, count + groups - 2)
 
-    def send(source, target, k, send_sem, recv_sem):
-        return pltpu.make_async_remote_copy(
-            src_ref=source, dst_ref=target, send_sem=send_sem.at[k], recv_sem=recv_sem.at[k],
-            device_id={"ctx": lax.rem(me + k, count)}, device_id_type=MESH,
-        )
-
-    def chunk(owner):
-        return pl.ds(pl.multiple_of(owner * width, 128), width)
-
     def gathered(k, slot):
-        to = lax.rem(me + k, count)
-        return (
-            send(st.at[:, chunk(to)], in_st.at[slot], k, st_send, st_recv),
-            send(raw.at[:, chunk(to)], in_raw.at[slot], k, raw_send, raw_recv),
-        )
-
-    def returned(k, slot, sums):
-        to = lax.rem(me + k, count)
-        if sums:
-            return send(out_s, in_s.at[slot], k, s_send, s_recv)
-        return send(out_c.at[to], in_c.at[slot], k, c_send, c_recv)
+        source = st.at[:, chunk(lax.rem(me + k, count), width)]
+        return peer_copy(source, in_st.at[slot], k, st_send, st_recv, count, me)
+
+    def returned(k, slot):
+        return peer_copy(out_c.at[lax.rem(me + k, count)], in_c.at[slot], k, c_send, c_recv, count, me)
 
     for k in range(1, count):
-        def start_one(k=k):
-            for copy in gathered(k, me):
-                copy.start()
-        guarded(lax.rem(me + k, count) < owners, start_one)
+        guarded(every, lax.rem(me + k, count) < owners, lambda k=k: gathered(k, me).start())
 
     def own():
-        in_st[me] = st[:, chunk(me)]
-        in_raw[me] = raw[:, chunk(me)]
-        for k in range(1, count):
-            for copy in gathered(k, lax.rem(me + count - k, count)):
-                copy.wait_recv()
-        rate = rates[:, chunk(me)]
+        in_st[me] = st[:, chunk(me, width)]
+        rate = rates[:, chunk(me, width)]
         fade = jnp.exp(-rate)
         over = jnp.exp(-float(length) * rate)
+        for k in range(1, count):
+            gathered(k, lax.rem(me + count - k, count)).wait_recv()
         carry = jnp.zeros(rate.shape, F32)
         residue = jnp.zeros(rate.shape, F32)
         for i in range(count):
@@ -265,34 +339,24 @@
         for i in reversed(range(count)):
             out_c[i, modes : 2 * modes] = carry
             carry = carry * over + in_st[i, modes : 2 * modes]
-        sums = in_raw[0]
-        for i in range(1, count):
-            sums = sums + in_raw[i]
-        residue = residue * amp[:, chunk(me)]
-        square = jnp.sum(jnp.sum(sums * sums, 0, keepdims=True), 1, keepdims=True) + jnp.sum(
-            jnp.sum(residue * residue, 0, keepdims=True), 1, keepdims=True
-        )
-        square = jnp.broadcast_to(square, (8, width))
+        residue = residue * amp[:, chunk(me, width)]
+        total = jnp.sum(jnp.sum(residue * residue, 0, keepdims=True), 1, keepdims=True)
+        total = jnp.broadcast_to(total, (8, width)) + square[...]
         for i in range(count):
-            out_c[i, 2 * modes : 2 * modes + 8] = square
-        out_s[...] = jnp.concatenate([sums, residue, jnp.zeros((8, width), F32)], 0).astype(BF16)
+            out_c[i, 2 * modes : 3 * modes] = residue
+            out_c[i, 3 * modes : 3 * modes + 8] = total
         for k in range(1, count):
-            returned(k, me, False).start()
-        for k in range(1, count):
-            returned(k, me, True).start()
+            returned(k, me).start()
         in_c[me] = out_c[me]
-        in_s[me] = out_s[...]
-
-    guarded(me < owners, own)
+
+    guarded(every, me < owners, own)
 
     for k in range(1, count):
         source = lax.rem(me + count - k, count)
-        def wait_carry(k=k, source=source):
-            returned(k, source, False).wait_recv()
-        guarded(source < owners, wait_carry)
-    total = in_c[0, 2 * modes : 2 * modes + 8]
+        guarded(every, source < owners, lambda k=k, source=source: returned(k, source).wait_recv())
+    total = in_c[0, 3 * modes : 3 * modes + 8]
     for i in range(1, owners):
-        total = total + in_c[i, 2 * modes : 2 * modes + 8]
+        total = total + in_c[i, 3 * modes : 3 * modes + 8]
     own_sq[...] = total
     in_sq[group] = total
 
@@ -306,11 +370,6 @@
         shared(k, group).start()
     for i in range(owners):
         carry_o[:, i * width : (i + 1) * width] = in_c[i, 0 : 2 * modes]
-    for k in range(1, count):
-        source = lax.rem(me + count - k, count)
-        def wait_sums(k=k, source=source):
-            returned(k, source, True).wait_recv()
-        guarded(source < owners, wait_sums)
     for k in range(1, groups):
         shared(k, lax.rem(group + groups - k, groups)).wait_recv()
     total = in_sq[0]
@@ -319,29 +378,21 @@
     factor = (1.0 / jnp.sqrt(total / entries + 1e-06))[0:1]
     for i in range(owners):
         cols = slice(i * width, (i + 1) * width)
-        block = in_s[i].astype(F32) * factor
+        block = sums[i].astype(F32) * factor
         short_o[:, cols] = block[0:taps]
-        medium_o[:, cols] = block[8 : 8 + lags]
-        residue_o[:, cols] = block[8 + lags : 8 + lags + modes]
+        medium_o[:, cols] = block[HALO : HALO + lags]
+        residue_o[:, cols] = in_c[i, 2 * modes : 3 * modes] * factor
     for k in range(1, count):
-        def wait_gather(k=k):
-            for copy in gathered(k, me):
-                copy.wait_send()
-        guarded(lax.rem(me + k, count) < owners, wait_gather)
-        def wait_return(k=k):
-            returned(k, me, False).wait_send()
-            returned(k, me, True).wait_send()
-        guarded(me < owners, wait_return)
+        guarded(every, lax.rem(me + k, count) < owners, lambda k=k: gathered(k, me).wait_send())
+        guarded(every, me < owners, lambda k=k: returned(k, me).wait_send())
     for k in range(1, groups):
         shared(k, group).wait_send()
 
 
-def exchange(st, raw, rates, amp, taps, lags, length):
+def exchange(st, sums, square, rates, amp, taps, lags, length):
     count, groups = lax.axis_size("ctx"), lax.axis_size("ch")
     modes, wide_c = rates.shape
-    owners = min(count, wide_c // 128)
-    width = wide_c // owners
-    rows = raw.shape[0]
+    owners, _, width = sums.shape
     entries = float((taps + lags + modes) * wide_c * groups)
     dma = pltpu.SemaphoreType.DMA
     vmem = pl.BlockSpec(memory_space=pltpu.VMEM)
@@ -353,24 +404,21 @@
             jax.ShapeDtypeStruct((modes, wide_c), F32),
             jax.ShapeDtypeStruct((2 * modes, wide_c), F32),
         ],
-        in_specs=[vmem] * 4,
+        in_specs=[vmem] * 5,
         out_specs=[vmem] * 4,
         scratch_shapes=[
             pltpu.VMEM((count, 3 * modes, width), F32),
-            pltpu.VMEM((count, rows, width), F32),
-            pltpu.VMEM((count, 2 * modes + 8, width), F32),
-            pltpu.VMEM((rows + modes + 8, width), BF16),
-            pltpu.VMEM((owners, 2 * modes + 8, width), F32),
-            pltpu.VMEM((owners, rows + modes + 8, width), BF16),
+            pltpu.VMEM((count, 3 * modes + 8, width), F32),
+            pltpu.VMEM((owners, 3 * modes + 8, width), F32),
             pltpu.VMEM((8, width), F32),
             pltpu.VMEM((groups, 8, width), F32),
         ]
-        + [dma((count,))] * 8
+        + [dma((count,))] * 4
         + [dma((groups,))] * 2,
         compiler_params=pltpu.CompilerParams(
             collective_id=0, has_side_effects=True, vmem_limit_bytes=48 << 20
         ),
-    )(st, raw, rates, amp)
+    )(st, sums, square, rates, amp)
 
 
 def body(
@@ -414,29 +462,52 @@
     params = pltpu.CompilerParams(dimension_semantics=("arbitrary",), vmem_limit_bytes=48 << 20)
     full = 2 * length
     long_f = np_hi_lo(transform(full, length))
-    long_i = np_hi_lo(transform(full, length).T * (2.0 / full))
-    fl, bl, st = pl.pallas_call(
+    long_i = np.asarray(transform(full, length).T * (2.0 / full), np.float32).astype(BF16)
+    long_in = (
+        query_long, key_long, value_long, grad_long, weights, decay_rates, jnp.asarray(long_f), jnp.asarray(long_i)
+    )
+    steps = channels // block
+    early = steps * 3 // 8
+    late = steps - early
+
+    def part_cols(rows, first):
+        return pl.BlockSpec((rows, block), lambda i: (0, i + first))
+
+    def long_specs(first):
+        return (
+            [part_cols(length, first)] * 4
+            + [part_cols(modes, first)] * 2
+            + [const(long_f.shape), const(long_i.shape)]
+        )
+
+    def long_shapes(number):
+        return [
+            jax.ShapeDtypeStruct((rows, number * block), F32) for rows in (length, length, 3 * modes)
+        ]
+
+    long_scratch = [pltpu.VMEM((length, block), F32)] * 3
+    fl_a, bl_a, st_a = pl.pallas_call(
         long_local_kernel,
-        grid=grid,
-        in_specs=[cols(length)] * 4 + [cols(modes)] * 2 + [const(long_f.shape), const(long_i.shape)],
+        grid=(early,),
+        in_specs=long_specs(0),
         out_specs=[cols(length), cols(length), cols(3 * modes)],
-        out_shape=[shape(length, F32), shape(length, F32), shape(3 * modes, F32)],
-        scratch_shapes=[pltpu.VMEM((length, block), F32)] * 3,
+        out_shape=long_shapes(early),
+        scratch_shapes=long_scratch,
         compiler_params=params,
-        cost_estimate=pl.CostEstimate(flops=20_000_000_000, bytes_accessed=8_000_000, transcendentals=0),
-    )(query_long, key_long, value_long, grad_long, weights, decay_rates, jnp.asarray(long_f), jnp.asarray(long_i))
+        cost_estimate=pl.CostEstimate(flops=10_000_000_000, bytes_accessed=4_000_000, transcendentals=0),
+    )(*long_in)
 
     part = length + lags
     part_f = np_hi_lo(transform(part, part))
-    part_i = np_hi_lo(transform(part, length).T * (2.0 / part))
+    part_i = np.asarray(transform(part, length).T * (2.0 / part), np.float32).astype(BF16)
     outs = pl.pallas_call(
         explicit_kernel,
         grid=grid,
         in_specs=[cols(length)] * 8
         + [cols(HALO + lags)] * 2
         + [cols(taps), cols(lags), const(part_f.shape), const(part_i.shape)],
-        out_specs=[cols(length)] * 6 + [cols(8 + lags)],
-        out_shape=[shape(length, BF16)] * 6 + [shape(8 + lags, F32)],
+        out_specs=[cols(length)] * 6 + [cols(HALO + lags)],
+        out_shape=[shape(length, BF16)] * 6 + [shape(HALO + lags, BF16)],
         compiler_params=params,
         cost_estimate=pl.CostEstimate(flops=20_000_000_000, bytes_accessed=16_000_000, transcendentals=0),
     )(
@@ -444,19 +515,54 @@
         query_medium, key_medium, value_medium, grad_medium,
         before, after, taps_short, taps_medium, jnp.asarray(part_f), jnp.asarray(part_i),
     )
+    count = lax.axis_size("ctx")
+    owners = min(count, channels // 128)
+    width = channels // owners
+    rows = HALO + lags
+    dma = pltpu.SemaphoreType.DMA
+    fl_b, bl_b, st_b, sums, square = pl.pallas_call(
+        functools.partial(long_sums_kernel, count, owners),
+        grid=(late,),
+        in_specs=long_specs(early) + [pl.BlockSpec(memory_space=pl.ANY)],
+        out_specs=[cols(length), cols(length), cols(3 * modes), const((owners, rows, width)), const((8, width))],
+        out_shape=long_shapes(late)
+        + [jax.ShapeDtypeStruct((owners, rows, width), BF16), jax.ShapeDtypeStruct((8, width), F32)],
+        scratch_shapes=long_scratch
+        + [
+            pltpu.VMEM((count, rows, width), BF16),
+            pltpu.VMEM((rows, width), BF16),
+            pltpu.VMEM((owners, rows, width), BF16),
+            dma,
+        ]
+        + [dma((count,))] * 4,
+        compiler_params=pltpu.CompilerParams(
+            dimension_semantics=("arbitrary",), vmem_limit_bytes=48 << 20,
+            collective_id=1, has_side_effects=True,
+        ),
+    )(*long_in, outs[6])
     short_g, medium_g, residue_g, carries = exchange(
-        st, outs[6], decay_rates, amplitudes, taps, lags, length
-    )
+        jnp.concatenate([st_a, st_b], 1), sums, square, decay_rates, amplitudes, taps, lags, length
+    )
+
+    def early_cols(rows):
+        return pl.BlockSpec((rows, block), lambda i: (0, jnp.minimum(i, early - 1)))
+
+    def late_cols(rows):
+        return pl.BlockSpec((rows, block), lambda i: (0, jnp.maximum(i - early, 0)))
+
     long_outs = pl.pallas_call(
-        long_final_kernel,
+        functools.partial(long_final_kernel, early),
         grid=grid,
-        in_specs=[cols(length)] * 5 + [cols(modes)] * 2 + [cols(2 * modes)],
+        in_specs=[cols(length)] * 3
+        + [early_cols(length), late_cols(length)] * 2
+        + [cols(modes)] * 2
+        + [cols(2 * modes)],
         out_specs=[cols(length)] * 3,
         out_shape=[shape(length, BF16)] * 3,
         scratch_shapes=[pltpu.VMEM((length, block), F32)] * 2,
         compiler_params=params,
         cost_estimate=pl.CostEstimate(flops=1_000_000_000, bytes_accessed=10_000_000, transcendentals=0),
-    )(key_long, value_long, grad_long, fl, bl, weights, decay_rates, carries)
+    )(key_long, value_long, grad_long, fl_a, fl_b, bl_a, bl_b, weights, decay_rates, carries)
     return (*outs[:6], *long_outs, short_g, medium_g, residue_g)
 
 

time: 146 us -> 130 us (0.89)
  the two profiles are of different devices: /device:TPU:0 before, /device:TPU:25 now
where the time goes in v2:
time: 130 us
  Pallas kernels  105 us (81%)
  waiting for transfers between devices  10.5 us (8%)
  starting transfers between devices  6.44 us (5%)
  other arithmetic  4.78 us (4%)
  local copies, waits for them, and re-layouts  2.35 us (2%)
    pallas_call x1, Pallas kernels, body(): pl.pallas_call(functools.partial(long_sums_kernel, count, owners), grid=(...  32.9 us
    pallas_call x1, Pallas kernels, exchange(): pl.pallas_call(functools.partial(exchange_kernel, count, groups, owners,...  29 us
    pallas_call x1, Pallas kernels, body(): pl.pallas_call(explicit_kernel, grid=grid, in_specs=[cols(length)] * 8 +...  21.5 us
    pallas_call x1, Pallas kernels, body(): pl.pallas_call(long_local_kernel, grid=(early,), in_specs=long_specs(0),...  11.4 us
    ppermute x2, waiting for transfers between devices, from_behind(): lax.ppermute(value, axis, [(source, source + steps) for source in range(f...  10.5 us
    pallas_call x1, Pallas kernels, body(): pl.pallas_call(functools.partial(long_final_kernel, early), grid=grid, in...  10.2 us
    ppermute x2, starting transfers between devices, from_behind(): lax.ppermute(value, axis, [(source, source + steps) for source in range(f...  6.44 us
    convert_element_type x4, other arithmetic, elementwise(): return (first.astype(F32) * second.astype(F32)).astype(BF16)  4.58 us
  transfers between devices with their start and end apart: 2, of which 1 were waited for; matrix products, arithmetic and copies ran while one was open for 2% of the time, Pallas kernels for 9%

profile of v2, /device:TPU:25, one launch (start us, length us, event | category | flops | bytes accessed | tf_op | source)
XLA Modules:
  0.0 129.8 jit_solution(4439089671469181280)
XLA Ops:
  0.6 0.0 copy-start.14
  0.7 0.9 multiply_convert_fusion.3
  1.6 0.0 copy-start.7
  1.6 0.0 copy-start.13
  1.6 1.5 %multiply_convert_fusion.1 = bf16[128,2048]{1,0:T(8,128)(2,1)S(1)} fusion(bf16[256,2048]{1,0:T(8,128)(2,1)} %vm.1, bf16[256,2048]{1,0:T(8,128)(2,1)} %km.1), kind=kLoop, calls=%fused_computation.1 | loop fusion | flops 1048576 | bytes 1572864 | tf_op jit(solution)/shard_map/convert_element_type | solution.py:24
  3.1 0.0 copy-start.5
  3.1 0.0 copy-start.6
  3.2 3.3 %collective-permute-start = (bf16[144,2048]{1,0:T(8,128)(2,1)S(1)}, bf16[144,2048]{1,0:T(8,128)(2,1)S(1)}, u32[]{:S(2)}, u32[]{:S(2)}) collective-permute-start(bf16[144,2048]{1,0:T(8,128)(2,1)S(1)} %pad_maximum_fusion), channel_id=1, source_target_pairs={{0,4},{4,8},{8,12},{12,16},{16,20},{20,24},{24,28},{1,5},{5,9},{9,... | collective-permute-start | bytes 1769480 | tf_op jit(solution)/shard_map/ppermute | solution.py:20
  6.4 0.0 copy-done.7
  6.5 0.9 multiply_convert_fusion.2
  7.3 0.0 copy-done.13
  7.3 0.0 copy-start.3
  7.3 0.0 copy-start.1
  7.4 0.0 copy-start.4
  7.4 1.3 %multiply_convert_fusion = bf16[128,2048]{1,0:T(8,128)(2,1)S(1)} fusion(bf16[256,2048]{1,0:T(8,128)(2,1)S(1)} %copy-done.13, bf16[256,2048]{1,0:T(8,128)(2,1)} %gm.1), kind=kLoop, calls=%fused_computation | loop fusion | flops 1048576 | bytes 1572864 | tf_op jit(solution)/shard_map/convert_element_type | solution.py:24
  8.7 0.0 copy-start
  8.8 3.2 %collective-permute-start.1 = (bf16[144,2048]{1,0:T(8,128)(2,1)S(1)}, bf16[144,2048]{1,0:T(8,128)(2,1)S(1)}, u32[]{:S(2)}, u32[]{:S(2)}) collective-permute-start(bf16[144,2048]{1,0:T(8,128)(2,1)S(1)} %pad_maximum_fusion.1), channel_id=1, source_target_pairs={{4,0},{8,4},{12,8},{16,12},{20,16},{24,20},{28,24},{5,1},{9,5},{13... | collective-permute-start | bytes 1769480 | tf_op jit(solution)/shard_map/ppermute | solution.py:20
  11.9 0.0 copy-done.14
  11.9 0.0 copy-done.3
  11.9 0.1 negate_sqrt_fusion
  12.0 0.0 copy-done.5
  12.1 0.0 copy-done.6
  12.1 0.0 copy-done.1
  12.1 0.0 copy-done.4
  12.1 0.0 copy-done
  12.1 0.0 copy-start.8
  12.1 0.0 copy-start.9
  12.1 0.0 copy-start.10
  12.1 0.0 copy-start.11
  12.1 0.0 copy-start.12
  12.2 11.4 %shard_map.284 = (f32[256,768]{1,0:T(8,128)S(1)}, f32[256,768]{1,0:T(8,128)S(1)}, f32[48,768]{1,0:T(8,128)S(1)}) custom-call(bf16[256,2048]{1,0:T(8,128)(2,1)S(1)} %copy-done.4, bf16[256,2048]{1,0:T(8,128)(2,1)S(1)} %copy-done, bf16[256,2048]{1,0:T(8,128)(2,1)S(1)} %copy-done.1, bf16[256,2048]{1,0:T(8,128)(2,1)} %g_ref.5, ...), custom_call_target="tpu_custom_call" | custom-call | flops 10000000000 | bytes 4000000 | tf_op jit(solution)/shard_map/pallas_call | solution.py:489
  23.5 0.0 collective-permute-done.before
  23.5 10.4 %collective-permute-done.1.after = bf16[144,2048]{1,0:T(8,128)(2,1)S(1)} collective-permute-done((bf16[144,2048]{1,0:T(8,128)(2,1)S(1)}, bf16[144,2048]{1,0:T(8,128)(2,1)S(1)}, u32[]{:S(2)}, u32[]{:S(2)}) %collective-permute-start.1) | collective-permute-done | bytes 589856 | tf_op jit(solution)/shard_map/ppermute | solution.py:20
  34.0 0.0 copy-done.8
  34.0 0.0 copy-done.9
  34.0 0.0 copy-done.10
  34.0 0.0 copy-done.11
  34.0 0.0 copy-done.12
  34.0 21.5 %shard_map.283 = (bf16[256,2048]{1,0:T(8,128)(2,1)}, bf16[256,2048]{1,0:T(8,128)(2,1)}, bf16[256,2048]{1,0:T(8,128)(2,1)}, bf16[256,2048]{1,0:T(8,128)(2,1)}, bf...) custom-call(bf16[256,2048]{1,0:T(8,128)(2,1)S(1)} %copy-done.7, ...), custom_call_target="tpu_custom_call" | custom-call | flops 20000000000 | bytes 16000000 | tf_op jit(solution)/shard_map/pallas_call | solution.py:503
  55.5 32.9 %shard_map.285 = (f32[256,1280]{1,0:T(8,128)}, f32[256,1280]{1,0:T(8,128)}, f32[48,1280]{1,0:T(8,128)S(1)}, bf16[8,144,256]{2,1,0:T(8,128)(2,1)S(1)}, f32[8,256]{1,0:T(8,128)S(1)}) custom-call(bf16[256,2048]{1,0:T(8,128)(2,1)S(1)} %copy-done.4, bf16[256,2048]{1,0:T(8,128)(2,1)S(1)} %copy-done, bf16[256,2048]{1,0:T(8,128)(2,1)S(1)} %copy-done.1, ...), custom_call_target="tpu_custom_call" | custom-call | tf_op jit(solution)/shard_map/pallas_call | solution.py:523
  88.3 0.0 copy-start.2
  88.4 29.0 %shard_map.286 = (f32[7,2048]{1,0:T(8,128)S(1)}, f32[128,2048]{1,0:T(8,128)S(1)}, f32[16,2048]{1,0:T(8,128)S(1)}, f32[32,2048]{1,0:T(8,128)S(1)}) custom-call(f32[48,2048]{1,0:T(8,128)S(1)} %pad_maximum_fusion.2.st, bf16[8,144,256]{2,1,0:T(8,128)(2,1)S(1)} %get-tuple-element.47.sums, f32[8,256]{1,0:T(8,128)S(1)} %get-tuple-element.48.square, ...), custom_call_target="tpu_custom_call" | custom-call | tf_op jit(solution)/shard_map/pallas_call | solution.py:399
  117.4 0.0 copy-done.2
  117.4 10.2 %shard_map.287 = (bf16[256,2048]{1,0:T(8,128)(2,1)}, bf16[256,2048]{1,0:T(8,128)(2,1)}, bf16[256,2048]{1,0:T(8,128)(2,1)}) custom-call(bf16[256,2048]{1,0:T(8,128)(2,1)S(1)} %copy-done, bf16[256,2048]{1,0:T(8,128)(2,1)S(1)} %copy-done.1, bf16[256,2048]{1,0:T(8,128)(2,1)S(1)} %copy-done.2, f32[256,768]{1,0:T(8,128)S(1)} %get-tuple-element.40.fl_a, ...), custom_call_target="tpu_custom_call" | custom-call | flops 1000000000 | bytes 10000000 | tf_op jit(solution)/shard_map/pallas_call | solution.py:553
  127.6 0.6 copy.35
  128.2 1.0 copy.36
  129.2 0.7 copy.37
  (3 shorter events, 0.1 us)
Async XLA Ops:
  0.6 11.3 %copy-start.14 = (f32[16,2048]{1,0:T(8,128)S(1)}, f32[16,2048]{1,0:T(8,128)}, u32[]{:S(2)}) copy-start(f32[16,2048]{1,0:T(8,128)} %param.34) | copy-start | bytes 393220
  1.6 4.9 %copy-start.7 = (bf16[256,2048]{1,0:T(8,128)(2,1)S(1)}, bf16[256,2048]{1,0:T(8,128)(2,1)}, u32[]{:S(2)}) copy-start(bf16[256,2048]{1,0:T(8,128)(2,1)} %qs.1) | copy-start | bytes 3145732
  1.6 5.7 %copy-start.13 = (bf16[256,2048]{1,0:T(8,128)(2,1)S(1)}, bf16[256,2048]{1,0:T(8,128)(2,1)}, u32[]{:S(2)}) copy-start(bf16[256,2048]{1,0:T(8,128)(2,1)} %qm.1) | copy-start | bytes 3145732
  3.1 9.0 %copy-start.5 = (bf16[2,512,256]{2,1,0:T(8,128)(2,1)S(1)}, bf16[2,512,256]{2,1,0:T(8,128)(2,1)}, u32[]{:S(2)}) copy-start(bf16[2,512,256]{2,1,0:T(8,128)(2,1)} %constant.10.clone.f_ref) | copy-start | bytes 1572868
  3.1 9.0 %copy-start.6 = (bf16[256,512]{1,0:T(8,128)(2,1)S(1)}, bf16[256,512]{1,0:T(8,128)(2,1)}, u32[]{:S(2)}) copy-start(bf16[256,512]{1,0:T(8,128)(2,1)} %constant.11.clone.i_ref) | copy-start | bytes 786436
  3.2 20.4 %collective-permute-start = (bf16[144,2048]{1,0:T(8,128)(2,1)S(1)}, bf16[144,2048]{1,0:T(8,128)(2,1)S(1)}, u32[]{:S(2)}, u32[]{:S(2)}) collective-permute-start(bf16[144,2048]{1,0:T(8,128)(2,1)S(1)} %pad_maximum_fusion), channel_id=1, source_target_pairs={{0,4},{4,8},{8,12},{12,16},{16,20},{20,24},{24,28},{1,5},{5,9},{9,... | collective-permute-start | bytes 1769480 | tf_op jit(solution)/shard_map/ppermute | solution.py:20
  7.3 4.6 %copy-start.3 = (f32[16,2048]{1,0:T(8,128)S(1)}, f32[16,2048]{1,0:T(8,128)}, u32[]{:S(2)}) copy-start(f32[16,2048]{1,0:T(8,128)} %d_ref.5) | copy-start | bytes 393220
  7.3 4.7 %copy-start.1 = (bf16[256,2048]{1,0:T(8,128)(2,1)S(1)}, bf16[256,2048]{1,0:T(8,128)(2,1)}, u32[]{:S(2)}) copy-start(bf16[256,2048]{1,0:T(8,128)(2,1)} %v_ref.5) | copy-start | bytes 3145732
  7.4 4.7 %copy-start.4 = (bf16[256,2048]{1,0:T(8,128)(2,1)S(1)}, bf16[256,2048]{1,0:T(8,128)(2,1)}, u32[]{:S(2)}) copy-start(bf16[256,2048]{1,0:T(8,128)(2,1)} %q_ref.3) | copy-start | bytes 3145732
  8.7 3.4 %copy-start = (bf16[256,2048]{1,0:T(8,128)(2,1)S(1)}, bf16[256,2048]{1,0:T(8,128)(2,1)}, u32[]{:S(2)}) copy-start(bf16[256,2048]{1,0:T(8,128)(2,1)} %k_ref.5) | copy-start | bytes 3145732
  8.8 25.2 %collective-permute-start.1 = (bf16[144,2048]{1,0:T(8,128)(2,1)S(1)}, bf16[144,2048]{1,0:T(8,128)(2,1)S(1)}, u32[]{:S(2)}, u32[]{:S(2)}) collective-permute-start(bf16[144,2048]{1,0:T(8,128)(2,1)S(1)} %pad_maximum_fusion.1), channel_id=1, source_target_pairs={{4,0},{8,4},{12,8},{16,12},{20,16},{24,20},{28,24},{5,1},{9,5},{13... | collective-permute-start | bytes 1769480 | tf_op jit(solution)/shard_map/ppermute | solution.py:20
  12.1 21.9 %copy-start.8 = (bf16[256,2048]{1,0:T(8,128)(2,1)S(1)}, bf16[256,2048]{1,0:T(8,128)(2,1)}, u32[]{:S(2)}) copy-start(bf16[256,2048]{1,0:T(8,128)(2,1)} %ks.1) | copy-start | bytes 3145732
  12.1 21.9 %copy-start.9 = (bf16[256,2048]{1,0:T(8,128)(2,1)S(1)}, bf16[256,2048]{1,0:T(8,128)(2,1)}, u32[]{:S(2)}) copy-start(bf16[256,2048]{1,0:T(8,128)(2,1)} %vs.1) | copy-start | bytes 3145732
  12.1 21.9 %copy-start.10 = (f32[7,2048]{1,0:T(8,128)S(1)}, f32[7,2048]{1,0:T(8,128)}, u32[]{:S(2)}) copy-start(f32[7,2048]{1,0:T(8,128)} %ts.1) | copy-start | bytes 172036
  12.1 21.9 %copy-start.11 = (bf16[2,384,384]{2,1,0:T(8,128)(2,1)S(1)}, bf16[2,384,384]{2,1,0:T(8,128)(2,1)}, u32[]{:S(2)}) copy-start(bf16[2,384,384]{2,1,0:T(8,128)(2,1)} %constant.12.clone.f_ref) | copy-start | bytes 1769476
  12.1 21.9 %copy-start.12 = (bf16[256,384]{1,0:T(8,128)(2,1)S(1)}, bf16[256,384]{1,0:T(8,128)(2,1)}, u32[]{:S(2)}) copy-start(bf16[256,384]{1,0:T(8,128)(2,1)} %constant.13.clone.i_ref) | copy-start | bytes 589828
  88.3 29.0 %copy-start.2 = (bf16[256,2048]{1,0:T(8,128)(2,1)S(1)}, bf16[256,2048]{1,0:T(8,128)(2,1)}, u32[]{:S(2)}) copy-start(bf16[256,2048]{1,0:T(8,128)(2,1)} %g_ref.5) | copy-start | bytes 3145732

commit v3 on v2

--- a/solution.py
+++ b/solution.py
@@ -98,7 +98,7 @@
             h_scr[pl.ds(pl.multiple_of(a * 8, 8), 8), cols] = jnp.sum(state, 0)
             return state * step
 
-        lax.fori_loop(0, tiles, filter_step, powers * w_ref[:, cols][:, None, :], unroll=4)
+        lax.fori_loop(0, tiles, filter_step, powers * w_ref[:, cols][:, None, :], unroll=8)
     ps = spectrum(f_ref, product)
     ss = spectrum(f_ref, signal)
     hs = wide(f_ref, h_scr[...])
@@ -121,11 +121,11 @@
             at = pl.ds(pl.multiple_of((tiles - 1 - a) * 8, 8), 8)
             return (states[0] * step + s_scr[at, cols][None], states[1] * step + h_scr[at, cols][None])
 
-        ends = lax.fori_loop(0, tiles, end_step, zeros, unroll=4)
-        st_ref[0:modes, cols] = jnp.sum(ends * falling, 1)
-        starts, lags = lax.fori_loop(0, tiles, start_step, (zeros, zeros), unroll=4)
-        st_ref[modes : 2 * modes, cols] = jnp.sum(starts * powers, 1)
-        st_ref[2 * modes : 3 * modes, cols] = jnp.sum(lags * powers, 1)
+        ends = lax.fori_loop(0, tiles, end_step, zeros, unroll=8)
+        st_ref[0:modes, cols] = jnp.sum(ends * falling, 1).astype(BF16)
+        starts, lags = lax.fori_loop(0, tiles, start_step, (zeros, zeros), unroll=8)
+        st_ref[modes : 2 * modes, cols] = jnp.sum(starts * powers, 1).astype(BF16)
+        st_ref[2 * modes : 3 * modes, cols] = jnp.sum(lags * powers, 1).astype(BF16)
 
 
 def explicit_kernel(
@@ -191,7 +191,7 @@
             b_scr[pl.ds(pl.multiple_of((tiles - 1 - a) * 8, 8), 8), cols] = jnp.sum(states[1], 0)
             return (states[0] * step, states[1] * step)
 
-        lax.fori_loop(0, tiles, one, (into, back), unroll=4)
+        lax.fori_loop(0, tiles, one, (into, back), unroll=8)
 
     def finish(fl_ref, bl_ref):
         backward = bl_ref[...] + b_scr[...]
@@ -331,20 +331,21 @@
         carry = jnp.zeros(rate.shape, F32)
         residue = jnp.zeros(rate.shape, F32)
         for i in range(count):
-            out_c[i, 0:modes] = carry
-            starts = in_st[i, modes : 2 * modes]
-            residue = residue + in_st[i, 2 * modes : 3 * modes] + carry * fade * starts
-            carry = carry * over + in_st[i, 0:modes]
+            out_c[i, 0:modes] = carry.astype(BF16)
+            starts = in_st[i, modes : 2 * modes].astype(F32)
+            residue = residue + in_st[i, 2 * modes : 3 * modes].astype(F32) + carry * fade * starts
+            carry = carry * over + in_st[i, 0:modes].astype(F32)
         carry = jnp.zeros(rate.shape, F32)
         for i in reversed(range(count)):
-            out_c[i, modes : 2 * modes] = carry
-            carry = carry * over + in_st[i, modes : 2 * modes]
+            out_c[i, modes : 2 * modes] = carry.astype(BF16)
+            carry = carry * over + in_st[i, modes : 2 * modes].astype(F32)
         residue = residue * amp[:, chunk(me, width)]
         total = jnp.sum(jnp.sum(residue * residue, 0, keepdims=True), 1, keepdims=True)
         total = jnp.broadcast_to(total, (8, width)) + square[...]
+        parts = [part.astype(F32) for part in hi_lo(total)]
+        shown = jnp.concatenate([residue] + parts, 0).astype(BF16)
         for i in range(count):
-            out_c[i, 2 * modes : 3 * modes] = residue
-            out_c[i, 3 * modes : 3 * modes + 8] = total
+            out_c[i, 2 * modes : 3 * modes + 16] = shown
         for k in range(1, count):
             returned(k, me).start()
         in_c[me] = out_c[me]
@@ -354,9 +355,10 @@
     for k in range(1, count):
         source = lax.rem(me + count - k, count)
         guarded(every, source < owners, lambda k=k, source=source: returned(k, source).wait_recv())
-    total = in_c[0, 3 * modes : 3 * modes + 8]
-    for i in range(1, owners):
-        total = total + in_c[i, 3 * modes : 3 * modes + 8]
+    total = jnp.zeros(own_sq.shape, F32)
+    for i in range(owners):
+        both = in_c[i, 3 * modes : 3 * modes + 16].astype(F32)
+        total = total + (both[0:8] + both[8:16])
     own_sq[...] = total
     in_sq[group] = total
 
@@ -369,7 +371,7 @@
     for k in range(1, groups):
         shared(k, group).start()
     for i in range(owners):
-        carry_o[:, i * width : (i + 1) * width] = in_c[i, 0 : 2 * modes]
+        carry_o[:, i * width : (i + 1) * width] = in_c[i, 0 : 2 * modes].astype(F32)
     for k in range(1, groups):
         shared(k, lax.rem(group + groups - k, groups)).wait_recv()
     total = in_sq[0]
@@ -381,7 +383,7 @@
         block = sums[i].astype(F32) * factor
         short_o[:, cols] = block[0:taps]
         medium_o[:, cols] = block[HALO : HALO + lags]
-        residue_o[:, cols] = in_c[i, 2 * modes : 3 * modes] * factor
+        residue_o[:, cols] = in_c[i, 2 * modes : 3 * modes].astype(F32) * factor
     for k in range(1, count):
         guarded(every, lax.rem(me + k, count) < owners, lambda k=k: gathered(k, me).wait_send())
         guarded(every, me < owners, lambda k=k: returned(k, me).wait_send())
@@ -407,9 +409,9 @@
         in_specs=[vmem] * 5,
         out_specs=[vmem] * 4,
         scratch_shapes=[
-            pltpu.VMEM((count, 3 * modes, width), F32),
-            pltpu.VMEM((count, 3 * modes + 8, width), F32),
-            pltpu.VMEM((owners, 3 * modes + 8, width), F32),
+            pltpu.VMEM((count, 3 * modes, width), BF16),
+            pltpu.VMEM((count, 3 * modes + 16, width), BF16),
+            pltpu.VMEM((owners, 3 * modes + 16, width), BF16),
             pltpu.VMEM((8, width), F32),
             pltpu.VMEM((groups, 8, width), F32),
         ]
@@ -482,7 +484,8 @@
 
     def long_shapes(number):
         return [
-            jax.ShapeDtypeStruct((rows, number * block), F32) for rows in (length, length, 3 * modes)
+            jax.ShapeDtypeStruct((rows, number * block), kind)
+            for rows, kind in ((length, F32), (length, F32), (3 * modes, BF16))
         ]
 
     long_scratch = [pltpu.VMEM((length, block), F32)] * 3

time: 130 us -> 122 us (0.938)
  the two profiles are of different devices: /device:TPU:25 before, /device:TPU:0 now
where the time goes in v3:
time: 122 us
  Pallas kernels  96.7 us (79%)
  waiting for transfers between devices  10.3 us (8%)
  starting transfers between devices  6.46 us (5%)
  other arithmetic  4.77 us (4%)
  local copies, waits for them, and re-layouts  2.35 us (2%)
    pallas_call x1, Pallas kernels, body(): pl.pallas_call(functools.partial(long_sums_kernel, count, owners), grid=(...  31.2 us
    pallas_call x1, Pallas kernels, exchange(): pl.pallas_call(functools.partial(exchange_kernel, count, groups, owners,...  23.2 us
    pallas_call x1, Pallas kernels, body(): pl.pallas_call(explicit_kernel, grid=grid, in_specs=[cols(length)] * 8 +...  21.5 us
    pallas_call x1, Pallas kernels, body(): pl.pallas_call(long_local_kernel, grid=(early,), in_specs=long_specs(0),...  10.9 us
    ppermute x2, waiting for transfers between devices, from_behind(): lax.ppermute(value, axis, [(source, source + steps) for source in range(f...  10.3 us
    pallas_call x1, Pallas kernels, body(): pl.pallas_call(functools.partial(long_final_kernel, early), grid=grid, in...  9.87 us
    ppermute x2, starting transfers between devices, from_behind(): lax.ppermute(value, axis, [(source, source + steps) for source in range(f...  6.46 us
    convert_element_type x4, other arithmetic, elementwise(): return (first.astype(F32) * second.astype(F32)).astype(BF16)  4.58 us
  transfers between devices with their start and end apart: 2, of which 1 were waited for; matrix products, arithmetic and copies ran while one was open for 2% of the time, Pallas kernels for 9%

profile of v3, /device:TPU:0, one launch (start us, length us, event | category | flops | bytes accessed | tf_op | source)
XLA Modules:
  0.0 121.5 jit_solution(534164764978320823)
XLA Ops:
  0.6 0.0 copy-start.14
  0.7 0.9 multiply_convert_fusion.3
  1.6 0.0 copy-start.7
  1.6 0.0 copy-start.13
  1.6 1.5 %multiply_convert_fusion.1 = bf16[128,2048]{1,0:T(8,128)(2,1)S(1)} fusion(bf16[256,2048]{1,0:T(8,128)(2,1)} %vm.1, bf16[256,2048]{1,0:T(8,128)(2,1)} %km.1), kind=kLoop, calls=%fused_computation.1 | loop fusion | flops 1048576 | bytes 1572864 | tf_op jit(solution)/shard_map/convert_element_type | solution.py:24
  3.1 0.0 copy-start.5
  3.1 0.0 copy-start.6
  3.2 5.0 %collective-permute-start = (bf16[144,2048]{1,0:T(8,128)(2,1)S(1)}, bf16[144,2048]{1,0:T(8,128)(2,1)S(1)}, u32[]{:S(2)}, u32[]{:S(2)}) collective-permute-start(bf16[144,2048]{1,0:T(8,128)(2,1)S(1)} %pad_maximum_fusion), channel_id=1, source_target_pairs={{0,4},{4,8},{8,12},{12,16},{16,20},{20,24},{24,28},{1,5},{5,9},{9,... | collective-permute-start | bytes 1769480 | tf_op jit(solution)/shard_map/ppermute | solution.py:20
  8.2 0.0 copy-done.7
  8.2 0.9 multiply_convert_fusion.2
  9.1 0.0 copy-done.13
  9.1 0.0 copy-start.3
  9.1 0.0 copy-start.1
  9.1 0.0 copy-start.4
  9.1 1.3 %multiply_convert_fusion = bf16[128,2048]{1,0:T(8,128)(2,1)S(1)} fusion(bf16[256,2048]{1,0:T(8,128)(2,1)S(1)} %copy-done.13, bf16[256,2048]{1,0:T(8,128)(2,1)} %gm.1), kind=kLoop, calls=%fused_computation | loop fusion | flops 1048576 | bytes 1572864 | tf_op jit(solution)/shard_map/convert_element_type | solution.py:24
  10.5 0.0 copy-start
  10.5 1.4 %collective-permute-start.1 = (bf16[144,2048]{1,0:T(8,128)(2,1)S(1)}, bf16[144,2048]{1,0:T(8,128)(2,1)S(1)}, u32[]{:S(2)}, u32[]{:S(2)}) collective-permute-start(bf16[144,2048]{1,0:T(8,128)(2,1)S(1)} %pad_maximum_fusion.1), channel_id=1, source_target_pairs={{4,0},{8,4},{12,8},{16,12},{20,16},{24,20},{28,24},{5,1},{9,5},{13... | collective-permute-start | bytes 1769480 | tf_op jit(solution)/shard_map/ppermute | solution.py:20
  11.9 0.0 copy-done.14
  12.0 0.0 copy-done.3
  12.0 0.1 negate_sqrt_fusion
  12.1 0.0 copy-done.5
  12.1 0.0 copy-done.6
  12.1 0.0 copy-done.1
  12.1 0.0 copy-done.4
  12.1 0.0 copy-done
  12.1 0.0 copy-start.8
  12.1 0.0 copy-start.9
  12.1 0.0 copy-start.10
  12.2 0.0 copy-start.11
  12.2 0.0 copy-start.12
  12.2 10.9 %shard_map.284 = (f32[256,768]{1,0:T(8,128)S(1)}, f32[256,768]{1,0:T(8,128)S(1)}, bf16[48,768]{1,0:T(8,128)(2,1)S(1)}) custom-call(bf16[256,2048]{1,0:T(8,128)(2,1)S(1)} %copy-done.4, bf16[256,2048]{1,0:T(8,128)(2,1)S(1)} %copy-done, bf16[256,2048]{1,0:T(8,128)(2,1)S(1)} %copy-done.1, bf16[256,2048]{1,0:T(8,128)(2,1)} %g_ref.5, ...), custom_call_target="tpu_custom_call" | custom-call | flops 10000000000 | bytes 4000000 | tf_op jit(solution)/shard_map/pallas_call | solution.py:492
  23.1 10.3 %collective-permute-done.before = bf16[144,2048]{1,0:T(8,128)(2,1)S(1)} collective-permute-done((bf16[144,2048]{1,0:T(8,128)(2,1)S(1)}, bf16[144,2048]{1,0:T(8,128)(2,1)S(1)}, u32[]{:S(2)}, u32[]{:S(2)}) %collective-permute-start) | collective-permute-done | bytes 589856 | tf_op jit(solution)/shard_map/ppermute | solution.py:20
  33.4 0.0 collective-permute-done.1.after
  33.4 0.0 copy-done.8
  33.4 0.0 copy-done.9
  33.4 0.0 copy-done.10
  33.4 0.0 copy-done.11
  33.4 0.0 copy-done.12
  33.4 21.5 %shard_map.283 = (bf16[256,2048]{1,0:T(8,128)(2,1)}, bf16[256,2048]{1,0:T(8,128)(2,1)}, bf16[256,2048]{1,0:T(8,128)(2,1)}, bf16[256,2048]{1,0:T(8,128)(2,1)}, bf...) custom-call(bf16[256,2048]{1,0:T(8,128)(2,1)S(1)} %copy-done.7, ...), custom_call_target="tpu_custom_call" | custom-call | flops 20000000000 | bytes 16000000 | tf_op jit(solution)/shard_map/pallas_call | solution.py:506
  54.9 31.2 %shard_map.285 = (f32[256,1280]{1,0:T(8,128)}, f32[256,1280]{1,0:T(8,128)}, bf16[48,1280]{1,0:T(8,128)(2,1)S(1)}, bf16[8,144,256]{2,1,0:T(8,128)(2,1)S(1)}, f32[8,256]{1,0:T(8,128)S(1)}) custom-call(bf16[256,2048]{1,0:T(8,128)(2,1)S(1)} %copy-done.4, bf16[256,2048]{1,0:T(8,128)(2,1)S(1)} %copy-done, bf16[256,2048]{1,0:T(8,128)(2,1)S(1)} %copy-done.1, ...), custom_call_target="tpu_custom_call" | custom-call | tf_op jit(solution)/shard_map/pallas_call | solution.py:526
  86.1 0.0 copy-start.2
  86.2 23.2 %shard_map.286 = (f32[7,2048]{1,0:T(8,128)S(1)}, f32[128,2048]{1,0:T(8,128)S(1)}, f32[16,2048]{1,0:T(8,128)S(1)}, f32[32,2048]{1,0:T(8,128)S(1)}) custom-call(bf16[48,2048]{1,0:T(8,128)(2,1)S(1)} %pad_maximum_fusion.2.st, bf16[8,144,256]{2,1,0:T(8,128)(2,1)S(1)} %get-tuple-element.47.sums, f32[8,256]{1,0:T(8,128)S(1)} %get-tuple-element.48.square, ...), custom_call_target="tpu_custom_call" | custom-call | tf_op jit(solution)/shard_map/pallas_call | solution.py:401
  109.4 0.0 copy-done.2
  109.4 9.9 %shard_map.287 = (bf16[256,2048]{1,0:T(8,128)(2,1)}, bf16[256,2048]{1,0:T(8,128)(2,1)}, bf16[256,2048]{1,0:T(8,128)(2,1)}) custom-call(bf16[256,2048]{1,0:T(8,128)(2,1)S(1)} %copy-done, bf16[256,2048]{1,0:T(8,128)(2,1)S(1)} %copy-done.1, bf16[256,2048]{1,0:T(8,128)(2,1)S(1)} %copy-done.2, f32[256,768]{1,0:T(8,128)S(1)} %get-tuple-element.40.fl_a, ...), custom_call_target="tpu_custom_call" | custom-call | flops 1000000000 | bytes 10000000 | tf_op jit(solution)/shard_map/pallas_call | solution.py:556
  119.3 0.6 copy.35
  119.9 1.0 copy.36
  120.9 0.7 copy.37
  (3 shorter events, 0.1 us)
Async XLA Ops:
  0.6 11.3 %copy-start.14 = (f32[16,2048]{1,0:T(8,128)S(1)}, f32[16,2048]{1,0:T(8,128)}, u32[]{:S(2)}) copy-start(f32[16,2048]{1,0:T(8,128)} %param.34) | copy-start | bytes 393220
  1.6 6.6 %copy-start.7 = (bf16[256,2048]{1,0:T(8,128)(2,1)S(1)}, bf16[256,2048]{1,0:T(8,128)(2,1)}, u32[]{:S(2)}) copy-start(bf16[256,2048]{1,0:T(8,128)(2,1)} %qs.1) | copy-start | bytes 3145732
  1.6 7.5 %copy-start.13 = (bf16[256,2048]{1,0:T(8,128)(2,1)S(1)}, bf16[256,2048]{1,0:T(8,128)(2,1)}, u32[]{:S(2)}) copy-start(bf16[256,2048]{1,0:T(8,128)(2,1)} %qm.1) | copy-start | bytes 3145732
  3.1 9.0 %copy-start.5 = (bf16[2,512,256]{2,1,0:T(8,128)(2,1)S(1)}, bf16[2,512,256]{2,1,0:T(8,128)(2,1)}, u32[]{:S(2)}) copy-start(bf16[2,512,256]{2,1,0:T(8,128)(2,1)} %constant.10.clone.f_ref) | copy-start | bytes 1572868
  3.1 9.0 %copy-start.6 = (bf16[256,512]{1,0:T(8,128)(2,1)S(1)}, bf16[256,512]{1,0:T(8,128)(2,1)}, u32[]{:S(2)}) copy-start(bf16[256,512]{1,0:T(8,128)(2,1)} %constant.11.clone.i_ref) | copy-start | bytes 786436
  3.2 30.2 %collective-permute-start = (bf16[144,2048]{1,0:T(8,128)(2,1)S(1)}, bf16[144,2048]{1,0:T(8,128)(2,1)S(1)}, u32[]{:S(2)}, u32[]{:S(2)}) collective-permute-start(bf16[144,2048]{1,0:T(8,128)(2,1)S(1)} %pad_maximum_fusion), channel_id=1, source_target_pairs={{0,4},{4,8},{8,12},{12,16},{16,20},{20,24},{24,28},{1,5},{5,9},{9,... | collective-permute-start | bytes 1769480 | tf_op jit(solution)/shard_map/ppermute | solution.py:20
  9.1 2.9 %copy-start.3 = (f32[16,2048]{1,0:T(8,128)S(1)}, f32[16,2048]{1,0:T(8,128)}, u32[]{:S(2)}) copy-start(f32[16,2048]{1,0:T(8,128)} %d_ref.5) | copy-start | bytes 393220
  9.1 3.0 %copy-start.1 = (bf16[256,2048]{1,0:T(8,128)(2,1)S(1)}, bf16[256,2048]{1,0:T(8,128)(2,1)}, u32[]{:S(2)}) copy-start(bf16[256,2048]{1,0:T(8,128)(2,1)} %v_ref.5) | copy-start | bytes 3145732
  9.1 3.0 %copy-start.4 = (bf16[256,2048]{1,0:T(8,128)(2,1)S(1)}, bf16[256,2048]{1,0:T(8,128)(2,1)}, u32[]{:S(2)}) copy-start(bf16[256,2048]{1,0:T(8,128)(2,1)} %q_ref.3) | copy-start | bytes 3145732
  10.5 1.7 %copy-start = (bf16[256,2048]{1,0:T(8,128)(2,1)S(1)}, bf16[256,2048]{1,0:T(8,128)(2,1)}, u32[]{:S(2)}) copy-start(bf16[256,2048]{1,0:T(8,128)(2,1)} %k_ref.5) | copy-start | bytes 3145732
  10.5 22.9 %collective-permute-start.1 = (bf16[144,2048]{1,0:T(8,128)(2,1)S(1)}, bf16[144,2048]{1,0:T(8,128)(2,1)S(1)}, u32[]{:S(2)}, u32[]{:S(2)}) collective-permute-start(bf16[144,2048]{1,0:T(8,128)(2,1)S(1)} %pad_maximum_fusion.1), channel_id=1, source_target_pairs={{4,0},{8,4},{12,8},{16,12},{20,16},{24,20},{28,24},{5,1},{9,5},{13... | collective-permute-start | bytes 1769480 | tf_op jit(solution)/shard_map/ppermute | solution.py:20
  12.1 21.3 %copy-start.8 = (bf16[256,2048]{1,0:T(8,128)(2,1)S(1)}, bf16[256,2048]{1,0:T(8,128)(2,1)}, u32[]{:S(2)}) copy-start(bf16[256,2048]{1,0:T(8,128)(2,1)} %ks.1) | copy-start | bytes 3145732
  12.1 21.3 %copy-start.9 = (bf16[256,2048]{1,0:T(8,128)(2,1)S(1)}, bf16[256,2048]{1,0:T(8,128)(2,1)}, u32[]{:S(2)}) copy-start(bf16[256,2048]{1,0:T(8,128)(2,1)} %vs.1) | copy-start | bytes 3145732
  12.1 21.3 %copy-start.10 = (f32[7,2048]{1,0:T(8,128)S(1)}, f32[7,2048]{1,0:T(8,128)}, u32[]{:S(2)}) copy-start(f32[7,2048]{1,0:T(8,128)} %ts.1) | copy-start | bytes 172036
  12.2 21.2 %copy-start.11 = (bf16[2,384,384]{2,1,0:T(8,128)(2,1)S(1)}, bf16[2,384,384]{2,1,0:T(8,128)(2,1)}, u32[]{:S(2)}) copy-start(bf16[2,384,384]{2,1,0:T(8,128)(2,1)} %constant.12.clone.f_ref) | copy-start | bytes 1769476
  12.2 21.2 %copy-start.12 = (bf16[256,384]{1,0:T(8,128)(2,1)S(1)}, bf16[256,384]{1,0:T(8,128)(2,1)}, u32[]{:S(2)}) copy-start(bf16[256,384]{1,0:T(8,128)(2,1)} %constant.13.clone.i_ref) | copy-start | bytes 589828
  86.1 23.3 %copy-start.2 = (bf16[256,2048]{1,0:T(8,128)(2,1)S(1)}, bf16[256,2048]{1,0:T(8,128)(2,1)}, u32[]{:S(2)}) copy-start(bf16[256,2048]{1,0:T(8,128)(2,1)} %g_ref.5) | copy-start | bytes 3145732
